TPU v7x, 1024 devices: a whole 8x8x8 slice. The times are simulated.
1024 devices in a mesh: img: 64 (over x_hi, y, core), txt: 16 (over x_lo, z).
Axes of the slice: x: 8 (x_hi: 4, x_lo: 2; x = x_hi * 2 + x_lo), y: 8, z: 8, core: 2. Of those that a mesh axis runs over, the one named last changes fastest.
Arguments:
- images: bfloat16 [24576, 512], P('img'), may hold values from -1 to 1
- texts: bfloat16 [24576, 512], P(('txt', 'img')), may hold values from -1 to 1
Outputs:
- grad_images: float32 [24576, 512], P(('img', 'txt'))
- grad_texts: float32 [24576, 512], P(('txt', 'img'))
All inputs are finite; a program needn't handle non-finite values.
Results may differ from a plain program's by a relative error of at most 0.0075.
Values may be sent and summed in bfloat16 or wider, within the bound.
No kernel may reach another device: no remote copies, remote signals or barrier semaphores. Data moves between devices by JAX's collectives and lax.ppermute only.
A program may use at most 32 MiB of HBM per device.

v0:
```python
import jax
import jax.numpy as jnp
from jax import lax
from jax.sharding import PartitionSpec as P

ROUNDS = 3


logit_scale = 30.0
mix_weight = 0.5
norm_eps = 1e-06
highest = lax.Precision.HIGHEST


def normalize(values):
    wide = values.astype(jnp.float32)
    length = jnp.sqrt(jnp.sum(wide * wide, axis=1, keepdims=True) + norm_eps)
    return (wide / length, length)


def project_back(grad, unit, length):
    along = jnp.sum(unit * grad, axis=1, keepdims=True)
    return (grad - unit * along) / length


def shards(images, texts):
    own_rows = texts.shape[0]
    img_block = images.shape[0]
    img_index = lax.axis_index("img")
    txt_index = lax.axis_index("txt")
    unit_img, len_img = normalize(images)
    img_bf = unit_img.astype(jnp.bfloat16)
    unit_txt, len_txt = normalize(texts)
    txt_bf = lax.all_gather(unit_txt.astype(jnp.bfloat16), "img", axis=0, tiled=True)
    txt_block = txt_bf.shape[0]
    total = float(img_block * lax.axis_size("img"))
    scores = logit_scale * lax.dot_general(
        img_bf, txt_bf, (((1,), (1,)), ((), ())), preferred_element_type=jnp.float32
    )
    kernel = jnp.exp(scores - logit_scale)
    row_weight = jnp.ones((img_block,), jnp.float32)
    col_scale = jnp.ones((txt_block,), jnp.float32)
    col_total = col_scale
    row_total = row_weight
    last_cols = col_scale
    for step in range(ROUNDS + 1):
        col_part = jnp.dot(row_weight, kernel, precision=highest)
        col_sum = lax.psum(col_part, "img")
        if step == 0:
            col_total = col_sum
        if step == ROUNDS:
            last_cols = col_sum
        else:
            col_scale = 1.0 / (total * col_sum)
            row_part = jnp.dot(kernel, col_scale, precision=highest)
            if step == 0:
                stats = jnp.stack([row_part, jnp.sum(kernel, axis=1)])
            else:
                stats = row_part[None, :]
            summed = lax.psum(stats, "txt")
            if step == 0:
                row_total = summed[1]
            row_weight = 1.0 / (total * summed[0])
    col_weight = 1.0 - mix_weight + mix_weight * total * col_scale * last_cols
    img_ids = img_index * img_block + jnp.arange(img_block, dtype=jnp.int32)
    txt_ids = txt_index * txt_block + jnp.arange(txt_block, dtype=jnp.int32)
    eye = (img_ids[:, None] == txt_ids[None, :]).astype(jnp.float32)
    target = (1.0 - mix_weight) * eye + mix_weight * total * row_weight[
        :, None
    ] * kernel * col_scale[None, :]
    grad_logit = 0.5 * (
        kernel / row_total[:, None]
        + col_weight[None, :] * kernel / col_total[None, :]
        - 2.0 * target
    )
    grad_logit = grad_logit.astype(jnp.bfloat16)
    g_img = lax.psum_scatter(
        logit_scale * jnp.dot(grad_logit, txt_bf, preferred_element_type=jnp.float32),
        "txt",
        scatter_dimension=0,
        tiled=True,
    )
    g_txt = lax.psum_scatter(
        logit_scale
        * lax.dot_general(
            grad_logit, img_bf, (((0,), (0,)), ((), ())), preferred_element_type=jnp.float32
        ),
        "img",
        scatter_dimension=0,
        tiled=True,
    )
    own_unit = lax.dynamic_slice_in_dim(unit_img, txt_index * own_rows, own_rows, 0)
    own_len = lax.dynamic_slice_in_dim(len_img, txt_index * own_rows, own_rows, 0)
    grad_images = project_back(g_img, own_unit, own_len)
    grad_texts = project_back(g_txt, unit_txt, len_txt)
    return (grad_images, grad_texts)


def solution(mesh):
    placed = (P("img", None), P(("txt", "img"), None))
    return jax.shard_map(
        shards,
        mesh=mesh,
        in_specs=placed,
        out_specs=(P(("img", "txt"), None), P(("txt", "img"), None)),
        check_vma=False,
    )
```

profile of v0, /device:TPU:1, one launch (start us, length us, event | category | flops | bytes accessed | tf_op | source)
XLA Modules:
  0.0 1034.5 jit_solution(1410420720086170660)
XLA Ops:
  8.7 1.4 fusion.24
  12.5 101.6 %all-gather.2.cloned.1.call-done = bf16[1536,512]{1,0:T(8,128)(2,1)} async-done(((bf16[24,512]{1,0:T(8,128)(2,1)}), bf16[1536,512]{1,0:T(8,128)(2,1)}) %all-gather.2.cloned.1.call-update) | async-done | bytes 1572880 | tf_op jit(solution)/shard_map/all_gather | solution.py:34
  114.2 2.5 fusion.25
  116.7 1.2 convolution_reduce_fusion.3
  117.9 140.1 %psum.49 = f32[1536]{0:T(1024)S(1)} all-reduce(f32[1536]{0:T(1024)S(1)} %convolution_reduce_fusion.3), channel_id=1, replica_groups=mesh['img'=64,'txt'=16] {'img'}, use_global_device_ids=true, to_apply=%region_2.0 | all-reduce | flops 1536 | bytes 12288 | tf_op jit(solution)/shard_map/psum | solution.py:48
  258.0 2.0 fusion.26
  260.1 28.5 %psum.50 = f32[2,384]{1,0:T(2,128)S(1)} all-reduce(f32[2,384]{1,0:T(2,128)S(1)} %pad_maximum_fusion), channel_id=1, replica_groups=mesh['img'=64,'txt'=16] {'txt'}, use_global_device_ids=true, to_apply=%region_4.0 | all-reduce | flops 768 | bytes 6144 | tf_op jit(solution)/shard_map/psum | solution.py:60
  288.6 1.2 convolution_reduce_fusion.2
  289.8 151.5 %psum.51 = f32[1536]{0:T(1024)S(1)} all-reduce(f32[1536]{0:T(1024)S(1)} %convolution_reduce_fusion.2), channel_id=1, replica_groups=mesh['img'=64,'txt'=16] {'img'}, use_global_device_ids=true, to_apply=%region_5.0 | all-reduce | flops 1536 | bytes 12288 | tf_op jit(solution)/shard_map/psum | solution.py:48
  441.4 2.0 fusion.27
  443.4 23.7 %psum.52 = f32[1,384]{1,0:T(1,128)S(1)} all-reduce(f32[1,384]{1,0:T(1,128)S(1)} %fusion.27), channel_id=1, replica_groups=mesh['img'=64,'txt'=16] {'txt'}, use_global_device_ids=true, to_apply=%region_6.0 | all-reduce | flops 384 | bytes 3072 | tf_op jit(solution)/shard_map/psum | solution.py:60
  467.1 1.2 convolution_reduce_fusion.1
  468.3 147.4 %psum.53 = f32[1536]{0:T(1024)S(1)} all-reduce(f32[1536]{0:T(1024)S(1)} %convolution_reduce_fusion.1), channel_id=1, replica_groups=mesh['img'=64,'txt'=16] {'img'}, use_global_device_ids=true, to_apply=%region_7.0 | all-reduce | flops 1536 | bytes 12288 | tf_op jit(solution)/shard_map/psum | solution.py:48
  615.7 2.0 fusion.28
  617.8 25.7 %psum.54 = f32[1,384]{1,0:T(1,128)S(1)} all-reduce(f32[1,384]{1,0:T(1,128)S(1)} %fusion.28), channel_id=1, replica_groups=mesh['img'=64,'txt'=16] {'txt'}, use_global_device_ids=true, to_apply=%region_8.0 | all-reduce | flops 384 | bytes 3072 | tf_op jit(solution)/shard_map/psum | solution.py:60
  643.5 1.2 convolution_reduce_fusion
  645.9 147.7 %psum.55 = f32[1536]{0:T(1024)S(1)} all-reduce(f32[1536]{0:T(1024)S(1)} %convolution_reduce_fusion), channel_id=1, replica_groups=mesh['img'=64,'txt'=16] {'img'}, use_global_device_ids=true, to_apply=%region_9.0 | all-reduce | flops 1536 | bytes 12288 | tf_op jit(solution)/shard_map/psum | solution.py:48
  793.6 1.9 multiply_convert_fusion
  795.6 1.7 convolution_multiply_fusion.2
  797.3 2.7 convolution_multiply_fusion
  800.3 54.5 %reduce-scatter.3.cloned.1.call-done = f32[24,512]{1,0:T(8,128)} async-done(((f32[384,512]{1,0:T(8,128)}), f32[24,512]{1,0:T(8,128)}) %reduce-scatter.3.cloned.1.call-update) | async-done | bytes 49168 | tf_op jit(solution)/shard_map/reduce_scatter | solution.py:77
  855.7 1.5 subtract_divide_fusion.1
  857.2 168.3 %reduce-scatter.5.cloned.1.call-done = f32[24,512]{1,0:T(8,128)} async-done(((f32[1536,512]{1,0:T(8,128)}), f32[24,512]{1,0:T(8,128)}) %reduce-scatter.5.cloned.1.call-update) | async-done | bytes 49168 | tf_op jit(solution)/shard_map/reduce_scatter | solution.py:83
  1026.5 1.5 subtract_divide_fusion
  (42 shorter events, 7.3 us)
Async XLA Ops:
  7.2 107.0 %all-gather.2.cloned.1.call-start = ((), (), s32[]{:S(2)}) async-start(), calls=%async_computation.2 | async-start | bytes 1597440 | tf_op jit(solution)/shard_map/all_gather | solution.py:34
  8.1 0.6 copy-start.4
  10.1 844.7 %reduce-scatter.3.cloned.1.call-start = ((), (), s32[]{:S(2)}) async-start(), calls=%async_computation.3 | async-start | bytes 835584 | tf_op jit(solution)/shard_map/reduce_scatter | solution.py:77
  12.5 104.2 %copy-start.2 = (f32[384]{0:T(512)}, f32[384]{0:T(512)S(1)}, u32[]{:S(2)}) copy-start(f32[384]{0:T(512)S(1)} %add_sqrt_fusion) | copy-start | bytes 4612
  793.6 2.0 copy-start.6
  795.6 1.8 copy-start
  795.6 1.8 copy-start.3
  797.3 228.2 %reduce-scatter.5.cloned.1.call-start = ((), (), s32[]{:S(2)}) async-start(), calls=%async_computation.4 | async-start | bytes 3194880 | tf_op jit(solution)/shard_map/reduce_scatter | solution.py:83
  800.1 225.4 %copy-start.1 = (bf16[24,512]{1,0:T(8,128)(2,1)S(1)}, bf16[24,512]{1,0:T(8,128)(2,1)}, u32[]{:S(2)}) copy-start(bf16[24,512]{1,0:T(8,128)(2,1)} %param.3) | copy-start | bytes 73732
  800.1 225.4 %copy-start.5 = (f32[24]{0:T(128)S(1)}, f32[24]{0:T(128)}, u32[]{:S(2)}) copy-start(f32[24]{0:T(128)} %copy-done.4) | copy-start | bytes 292
Sparse Core Ops, SparseCore 0:
  13.1 101.0 all-gather.1
  797.4 57.3 reduce-scatter.2
  861.7 163.7 reduce-scatter.4
where the time goes:
time: 1040 us; the launch traced here: 1030 us
  blocking collectives  665 us (64%)
  waiting for transfers between devices  324 us (31%)
  matrix products  17.9 us (2%)
  between operations  14 us (1%)
  other arithmetic  12.3 us (1%)
    psum x4, blocking collectives, shards(): col_sum = lax.psum(col_part, 'img')  587 us
    reduce_scatter x1, waiting for transfers between devices, shards(): lax.psum_scatter(logit_scale * lax.dot_general(grad_logit, img_bf, (((0,)...  168 us
    all_gather x1, waiting for transfers between devices, shards(): lax.all_gather(unit_txt.astype(jnp.bfloat16), 'img', axis=0, tiled=True)  102 us
    psum x3, blocking collectives, shards(): summed = lax.psum(stats, 'txt')  77.9 us
    reduce_scatter x1, waiting for transfers between devices, shards(): lax.psum_scatter(logit_scale * jnp.dot(grad_logit, txt_bf, preferred_elem...  54.5 us
  transfers between devices with their start and end apart: 3, of which 3 were waited for; matrix products, arithmetic and copies ran while one was open for 1% of the time, Pallas kernels for 0%

commit v1 on v0

v1 whole, which is shorter than its diff:
```python
import jax
import jax.numpy as jnp
from jax import lax
from jax.sharding import Mesh, PartitionSpec as P

ROUNDS = 3
CORES = 2

logit_scale = 30.0
mix_weight = 0.5
norm_eps = 1e-06


def normalize(values):
    wide = values.astype(jnp.float32)
    length = jnp.sqrt(jnp.sum(wide * wide, axis=1, keepdims=True) + norm_eps)
    return (wide / length, length)


def project_back(grad, unit, length):
    along = jnp.sum(unit * grad, axis=1, keepdims=True)
    return (grad - unit * along) / length


def share(values, axes):
    count = lax.axis_size(axes)
    copies = jnp.broadcast_to(values[None], (count,) + values.shape)
    return lax.all_to_all(copies, axes, 0, 0, tiled=True)


def total_over(values, axes):
    return jnp.sum(share(values, axes), axis=0)


def scatter_sum(values, axes):
    count = lax.axis_size(axes)
    parts = values.astype(jnp.bfloat16).reshape(count, -1, values.shape[1])
    return jnp.sum(lax.all_to_all(parts, axes, 0, 0, tiled=True).astype(jnp.float32), axis=0)


def shards(images, texts):
    own = texts.shape[0]
    p_index = lax.axis_index("p")
    c_index = lax.axis_index("c")
    t_index = lax.axis_index("t")
    unit_txt, len_txt = normalize(texts)
    txt_bf = share(unit_txt.astype(jnp.bfloat16), "p").reshape(-1, texts.shape[1])
    both = lax.all_gather(images, "c", axis=0, tiled=True)
    unit_img, len_img = normalize(both)
    img_bf = unit_img.astype(jnp.bfloat16)
    n_img, n_txt = img_bf.shape[0], txt_bf.shape[0]
    total = float(n_img * lax.axis_size("p"))
    scores = logit_scale * lax.dot_general(
        img_bf, txt_bf, (((1,), (1,)), ((), ())), preferred_element_type=jnp.float32
    )
    kernel = jnp.exp(scores - logit_scale)
    col_total = total_over(jnp.sum(kernel, axis=0), "p")
    col_sum = col_total
    for step in range(ROUNDS):
        col_scale = 1.0 / (total * col_sum)
        row_part = jnp.sum(kernel * col_scale[None, :], axis=1)
        if step == 0:
            stats = total_over(jnp.stack([row_part, jnp.sum(kernel, axis=1)]), ("c", "t"))
            row_sum, row_total = stats[0], stats[1]
        else:
            row_sum = total_over(row_part, ("c", "t"))
        row_weight = 1.0 / (total * row_sum)
        col_sum = total_over(jnp.sum(kernel * row_weight[:, None], axis=0), "p")
    col_weight = 1.0 - mix_weight + mix_weight * total * col_scale * col_sum
    img_ids = p_index * n_img + jnp.arange(n_img, dtype=jnp.int32)
    place = jnp.arange(n_txt, dtype=jnp.int32)
    txt_ids = t_index * (n_txt * CORES) + (place // own * CORES + c_index) * own + place % own
    eye = (img_ids[:, None] == txt_ids[None, :]).astype(jnp.float32)
    target = (1.0 - mix_weight) * eye + mix_weight * total * row_weight[
        :, None
    ] * kernel * col_scale[None, :]
    grad_logit = 0.5 * (
        kernel / row_total[:, None]
        + col_weight[None, :] * kernel / col_total[None, :]
        - 2.0 * target
    )
    grad_logit = grad_logit.astype(jnp.bfloat16)
    g_img = scatter_sum(
        logit_scale * jnp.dot(grad_logit, txt_bf, preferred_element_type=jnp.float32), ("c", "t")
    )
    g_txt = scatter_sum(
        logit_scale
        * lax.dot_general(
            grad_logit, img_bf, (((0,), (0,)), ((), ())), preferred_element_type=jnp.float32
        ),
        "p",
    )
    first = c_index * (n_img // CORES) + t_index * own
    own_unit = lax.dynamic_slice_in_dim(unit_img, first, own, 0)
    own_len = lax.dynamic_slice_in_dim(len_img, first, own, 0)
    grad_images = project_back(g_img, own_unit, own_len)
    grad_texts = project_back(g_txt, unit_txt, len_txt)
    return (grad_images, grad_texts)


def solution(mesh):
    n_img, n_txt = mesh.devices.shape
    split = Mesh(mesh.devices.reshape(n_img // CORES, CORES, n_txt), ("p", "c", "t"))
    return jax.shard_map(
        shards,
        mesh=split,
        in_specs=(P(("p", "c"), None), P(("t", "p", "c"), None)),
        out_specs=(P(("p", "c", "t"), None), P(("t", "p", "c"), None)),
        check_vma=False,
    )
```

time: 1040 us -> 227 us (0.22)
  blocking collectives: 665 us -> 110 us
  waiting for transfers between devices: 324 us -> 62.8 us
  starting transfers between devices: 0.12 us -> 33.2 us
  between operations: 14 us -> 0.88 us
  matrix products: 17.9 us -> 6.74 us
    psum x7 -> x0, blocking collectives: 665 us -> none  [the longest x4 587 us: shards(): col_sum = lax.psum(col_part, 'img')]
    reduce_scatter x2 -> x0, waiting for transfers between devices: 223 us -> none  [the longest x1 168 us: shards(): lax.psum_scatter(logit_scale * lax.dot_general(grad_logit, img_bf, (((0,)...]
    all_to_all x0 -> x6, blocking collectives: none -> 103 us  [share(): return lax.all_to_all(copies, axes, 0, 0, tiled=True)]
    all_gather x1 -> x0, waiting for transfers between devices: 102 us -> none  [shards(): lax.all_gather(unit_txt.astype(jnp.bfloat16), 'img', axis=0, tiled=True)]
    all_to_all x0 -> x4, waiting for transfers between devices: none -> 62.8 us  [the longest x2 34.6 us: scatter_sum(): lax.all_to_all(parts, axes, 0, 0, tiled=True).astype(jnp.float32)]
    all_to_all x0 -> x4, starting transfers between devices: none -> 33.2 us  [the longest x2 17.3 us: share(): return lax.all_to_all(copies, axes, 0, 0, tiled=True)]
    dot_general x7 -> x0, matrix products: 11 us -> none  [the longest x3 6.1 us: shards(): row_part = jnp.dot(kernel, col_scale, precision=highest)]
  transfers between devices with their start and end apart: 3 -> 4, of which waited for: 3 -> 4; matrix products, arithmetic and copies ran while one was open for 1% -> 2% of each run, Pallas kernels for 0% -> 0%
where the time goes in v1:
time: 227 us; the launch traced here: 226 us
  blocking collectives  110 us (48%)
  waiting for transfers between devices  62.8 us (28%)
  starting transfers between devices  33.2 us (15%)
  other arithmetic  10.3 us (5%)
  matrix products  6.74 us (3%)
  local copies, waits for them, and re-layouts  2.92 us (1%)
    all_to_all x6, blocking collectives, share(): return lax.all_to_all(copies, axes, 0, 0, tiled=True)  103 us
    all_to_all x2, waiting for transfers between devices, scatter_sum(): lax.all_to_all(parts, axes, 0, 0, tiled=True).astype(jnp.float32)  34.6 us
    all_to_all x2, waiting for transfers between devices, share(): return lax.all_to_all(copies, axes, 0, 0, tiled=True)  28.1 us
    all_to_all x2, starting transfers between devices, share(): return lax.all_to_all(copies, axes, 0, 0, tiled=True)  17.3 us
    all_to_all x2, starting transfers between devices, scatter_sum(): lax.all_to_all(parts, axes, 0, 0, tiled=True).astype(jnp.float32)  15.9 us
    all_gather x1, blocking collectives, shards(): both = lax.all_gather(images, 'c', axis=0, tiled=True)  6.64 us
  transfers between devices with their start and end apart: 4, of which 4 were waited for; matrix products, arithmetic and copies ran while one was open for 2% of the time, Pallas kernels for 0%

profile of v1, /device:TPU:1, one launch (start us, length us, event | category | flops | bytes accessed | tf_op | source)
XLA Modules:
  0.0 226.3 jit_solution(4622750457192436216)
XLA Ops:
  0.6 0.9 fusion.3
  2.4 0.9 broadcast_in_dim.16
  3.3 13.4 %all-to-all-start = ((bf16[32,24,512]{2,1,0:T(8,128)(2,1)}), bf16[32,24,512]{2,1,0:T(8,128)(2,1)S(1)}, u32[]{:S(2)}, u32[]{:S(2)}) async-start(bf16[32,24,512]{2,1,0:T(8,128)(2,1)} %broadcast_in_dim.16), calls=%async_computation | async-start | bytes 1572864 | tf_op jit(solution)/shard_map/all_to_all | solution.py:28
  16.7 6.6 %all_gather.3 = bf16[768,512]{1,0:T(8,128)(2,1)S(1)} all-gather(bf16[384,512]{1,0:T(8,128)(2,1)S(1)} %copy-done.3), channel_id=1, replica_groups=mesh['p'=32,'c'=2,'t'=16] {'c'}, dimensions={0}, use_global_device_ids=true | all-gather | bytes 1179648 | tf_op jit(solution)/shard_map/all_gather | solution.py:48
  23.6 16.7 %all-to-all-done = bf16[32,24,512]{2,1,0:T(8,128)(2,1)S(1)} async-done(((bf16[32,24,512]{2,1,0:T(8,128)(2,1)}), bf16[32,24,512]{2,1,0:T(8,128)(2,1)S(1)}, u32[]{:S(2)}, u32[]{:S(2)}) %all-to-all-start) | async-done | bytes 786464 | tf_op jit(solution)/shard_map/all_to_all | solution.py:28
  41.2 2.1 fusion.17
  43.3 19.4 %all_to_all.56 = f32[32,1,768]{2,1,0:T(1,128)S(1)} all-to-all(f32[32,1,768]{2,1,0:T(1,128)S(1)} %broadcast_in_dim.17), channel_id=1, replica_groups=mesh['p'=32,'c'=2,'t'=16] {'p'}, dimensions={0} | all-to-all | bytes 196608 | tf_op jit(solution)/shard_map/all_to_all | solution.py:28
  63.3 28.6 %all_to_all.57 = f32[32,2,768]{2,1,0:T(2,128)S(1)} all-to-all(f32[32,2,768]{2,1,0:T(2,128)S(1)} %broadcast_in_dim.18), channel_id=1, replica_groups=mesh['p'=32,'c'=2,'t'=16] {'c','t'}, dimensions={0} | all-to-all | bytes 393216 | tf_op jit(solution)/shard_map/all_to_all | solution.py:28
  92.3 14.5 %all_to_all.58 = f32[32,1,768]{2,1,0:T(1,128)S(1)} all-to-all(f32[32,1,768]{2,1,0:T(1,128)S(1)} %broadcast_in_dim.19), channel_id=1, replica_groups=mesh['p'=32,'c'=2,'t'=16] {'p'}, dimensions={0} | all-to-all | bytes 196608 | tf_op jit(solution)/shard_map/all_to_all | solution.py:28
  107.2 13.0 %all_to_all.59 = f32[32,1,768]{2,1,0:T(1,128)S(1)} all-to-all(f32[32,1,768]{2,1,0:T(1,128)S(1)} %broadcast_in_dim.20), channel_id=1, replica_groups=mesh['p'=32,'c'=2,'t'=16] {'c','t'}, dimensions={0} | all-to-all | bytes 196608 | tf_op jit(solution)/shard_map/all_to_all | solution.py:28
  120.6 14.4 %all_to_all.60 = f32[32,1,768]{2,1,0:T(1,128)S(1)} all-to-all(f32[32,1,768]{2,1,0:T(1,128)S(1)} %broadcast_in_dim.21), channel_id=1, replica_groups=mesh['p'=32,'c'=2,'t'=16] {'p'}, dimensions={0} | all-to-all | bytes 196608 | tf_op jit(solution)/shard_map/all_to_all | solution.py:28
  135.4 12.9 %all_to_all.61 = f32[32,1,768]{2,1,0:T(1,128)S(1)} all-to-all(f32[32,1,768]{2,1,0:T(1,128)S(1)} %broadcast_in_dim.22), channel_id=1, replica_groups=mesh['p'=32,'c'=2,'t'=16] {'c','t'}, dimensions={0} | all-to-all | bytes 196608 | tf_op jit(solution)/shard_map/all_to_all | solution.py:28
  149.3 3.8 %all-to-all-start.7 = ((f32[32,1,768]{2,1,0:T(1,128)}), f32[32,1,768]{2,1,0:T(1,128)S(1)}, u32[]{:S(2)}, u32[]{:S(2)}) async-start(f32[32,1,768]{2,1,0:T(1,128)} %broadcast_in_dim.23), calls=%async_computation.7 | async-start | bytes 196608 | tf_op jit(solution)/shard_map/all_to_all | solution.py:28
  153.2 11.4 %all-to-all-done.7 = f32[32,1,768]{2,1,0:T(1,128)S(1)} async-done(((f32[32,1,768]{2,1,0:T(1,128)}), f32[32,1,768]{2,1,0:T(1,128)S(1)}, u32[]{:S(2)}, u32[]{:S(2)}) %all-to-all-start.7) | async-done | bytes 98336 | tf_op jit(solution)/shard_map/all_to_all | solution.py:28
  164.7 1.3 multiply_convert_fusion
  166.1 1.8 multiply_convert_fusion.1
  167.8 3.9 %all-to-all-start.9 = ((bf16[32,24,512]{2,1,0:T(8,128)(2,1)}), bf16[32,24,512]{2,1,0:T(8,128)(2,1)S(1)}, u32[]{:S(2)}, u32[]{:S(2)}) async-start(bf16[32,24,512]{2,1,0:T(8,128)(2,1)} %bitcast.2), calls=%async_computation.9 | async-start | bytes 1572864 | tf_op jit(solution)/shard_map/all_to_all | solution.py:38
  171.8 2.9 %multiply_convert_fusion.2 = bf16[768,512]{1,0:T(8,128)(2,1)} fusion(bf16[768,768]{1,0:T(8,128)(2,1)} %copy-done, bf16[768,512]{1,0:T(8,128)(2,1)S(1)} %bitcast.8), kind=kOutput, calls=%fused_computation.14 | convolution fusion | flops 604766208 | bytes 2752512 | tf_op jit(solution)/shard_map/dot_general | solution.py:84
  174.7 15.9 %all-to-all-done.9 = bf16[32,24,512]{2,1,0:T(8,128)(2,1)S(1)} async-done(((bf16[32,24,512]{2,1,0:T(8,128)(2,1)}), bf16[32,24,512]{2,1,0:T(8,128)(2,1)S(1)}, u32[]{:S(2)}, u32[]{:S(2)}) %all-to-all-start.9) | async-done | bytes 786464 | tf_op jit(solution)/shard_map/all_to_all | solution.py:38
  190.6 12.0 %all-to-all-start.8 = ((bf16[32,24,512]{2,1,0:T(8,128)(2,1)}), bf16[32,24,512]{2,1,0:T(8,128)(2,1)S(1)}, u32[]{:S(2)}, u32[]{:S(2)}) async-start(bf16[32,24,512]{2,1,0:T(8,128)(2,1)} %bitcast.1), calls=%async_computation.8 | async-start | bytes 1572864 | tf_op jit(solution)/shard_map/all_to_all | solution.py:38
  202.7 1.4 convert_divide_fusion
  205.1 18.7 %all-to-all-done.8 = bf16[32,24,512]{2,1,0:T(8,128)(2,1)S(1)} async-done(((bf16[32,24,512]{2,1,0:T(8,128)(2,1)}), bf16[32,24,512]{2,1,0:T(8,128)(2,1)S(1)}, u32[]{:S(2)}, u32[]{:S(2)}) %all-to-all-start.8) | async-done | bytes 786464 | tf_op jit(solution)/shard_map/all_to_all | solution.py:38
  223.9 0.9 multiply_reduce_fusion.7
  224.8 1.5 subtract_divide_fusion.1
  (50 shorter events, 6.3 us)
Async XLA Ops:
  0.6 16.1 %copy-start.3 = (bf16[384,512]{1,0:T(8,128)(2,1)S(1)}, bf16[384,512]{1,0:T(8,128)(2,1)}, u32[]{:S(2)}) copy-start(bf16[384,512]{1,0:T(8,128)(2,1)} %param.2) | copy-start | bytes 1179652
  3.3 37.0 %all-to-all-start = ((bf16[32,24,512]{2,1,0:T(8,128)(2,1)}), bf16[32,24,512]{2,1,0:T(8,128)(2,1)S(1)}, u32[]{:S(2)}, u32[]{:S(2)}) async-start(bf16[32,24,512]{2,1,0:T(8,128)(2,1)} %broadcast_in_dim.16), calls=%async_computation | async-start | bytes 1572864 | tf_op jit(solution)/shard_map/all_to_all | solution.py:28
  40.3 0.9 copy-start.1
  149.3 15.3 %all-to-all-start.7 = ((f32[32,1,768]{2,1,0:T(1,128)}), f32[32,1,768]{2,1,0:T(1,128)S(1)}, u32[]{:S(2)}, u32[]{:S(2)}) async-start(f32[32,1,768]{2,1,0:T(1,128)} %broadcast_in_dim.23), calls=%async_computation.7 | async-start | bytes 196608 | tf_op jit(solution)/shard_map/all_to_all | solution.py:28
  166.0 1.8 copy-start
  166.1 5.7 %copy-start.2 = (bf16[32,24,512]{2,1,0:T(8,128)(2,1)S(1)}, bf16[32,24,512]{2,1,0:T(8,128)(2,1)}, u32[]{:S(2)}) copy-start(bf16[32,24,512]{2,1,0:T(8,128)(2,1)} %copy-done.1) | copy-start | bytes 2359300
  167.8 22.8 %all-to-all-start.9 = ((bf16[32,24,512]{2,1,0:T(8,128)(2,1)}), bf16[32,24,512]{2,1,0:T(8,128)(2,1)S(1)}, u32[]{:S(2)}, u32[]{:S(2)}) async-start(bf16[32,24,512]{2,1,0:T(8,128)(2,1)} %bitcast.2), calls=%async_computation.9 | async-start | bytes 1572864 | tf_op jit(solution)/shard_map/all_to_all | solution.py:38
  190.6 13.6 %copy-start.4 = (bf16[24,512]{1,0:T(8,128)(2,1)S(1)}, bf16[24,512]{1,0:T(8,128)(2,1)}, u32[]{:S(2)}) copy-start(bf16[24,512]{1,0:T(8,128)(2,1)} %param.3) | copy-start | bytes 73732
  190.6 33.2 %all-to-all-start.8 = ((bf16[32,24,512]{2,1,0:T(8,128)(2,1)}), bf16[32,24,512]{2,1,0:T(8,128)(2,1)S(1)}, u32[]{:S(2)}, u32[]{:S(2)}) async-start(bf16[32,24,512]{2,1,0:T(8,128)(2,1)} %bitcast.1), calls=%async_computation.8 | async-start | bytes 1572864 | tf_op jit(solution)/shard_map/all_to_all | solution.py:38

commit v2 on v1

v2 whole, which is shorter than its diff:
```python
import jax
import jax.numpy as jnp
from jax import lax
from jax.sharding import Mesh, PartitionSpec as P

ROUNDS = 3
CORES = 2
NEAR = 2
FAR = 2

logit_scale = 30.0
mix_weight = 0.5
norm_eps = 1e-06


def normalize(values):
    wide = values.astype(jnp.float32)
    length = jnp.sqrt(jnp.sum(wide * wide, axis=1, keepdims=True) + norm_eps)
    return (wide / length, length)


def project_back(grad, unit, length):
    along = jnp.sum(unit * grad, axis=1, keepdims=True)
    return (grad - unit * along) / length


def exchange(parts, axes):
    return lax.all_to_all(parts, axes, 0, 0, tiled=True)


def share(values, axes):
    return exchange(jnp.broadcast_to(values[None], (lax.axis_size(axes),) + values.shape), axes)


def total_over(values, axes):
    return jnp.sum(share(values, axes), axis=0)


def scatter_sum(values, axes):
    return jnp.sum(exchange(values.astype(jnp.bfloat16), axes).astype(jnp.float32), axis=0)


def keep_half(values, axis, dim, dtype):
    me = lax.axis_index(axis)
    half = values.shape[dim] // 2
    mine = lax.dynamic_slice_in_dim(values, me * half, half, dim)
    other = lax.dynamic_slice_in_dim(values, (1 - me) * half, half, dim)
    return mine + lax.ppermute(other.astype(dtype), axis, [(0, 1), (1, 0)]).astype(jnp.float32)


def shards(images, texts):
    own, width = texts.shape
    p_index = lax.axis_index("p")
    c_index = lax.axis_index("c")
    t_index = lax.axis_index(("x", "zh", "zl"))
    rows = ("c", "x", "zh", "zl")
    raw_txt = share(texts, "p").reshape(-1, width)
    both = lax.all_gather(images, "c", axis=0, tiled=True)
    n_img, n_txt = both.shape[0], raw_txt.shape[0]
    total = float(n_img * lax.axis_size("p"))
    img_ids = p_index * n_img + jnp.arange(n_img, dtype=jnp.int32)
    place = jnp.arange(n_txt, dtype=jnp.int32)
    txt_ids = t_index * (n_txt * CORES) + (place // own * CORES + c_index) * own + place % own
    both, img_ids, txt_ids = lax.optimization_barrier((both, img_ids, txt_ids))
    img_bf = normalize(both)[0].astype(jnp.bfloat16)
    txt_bf = normalize(raw_txt)[0].astype(jnp.bfloat16)
    scores = logit_scale * lax.dot_general(
        txt_bf, img_bf, (((1,), (1,)), ((), ())), preferred_element_type=jnp.float32
    )
    kernel = jnp.exp(scores - logit_scale)
    col_total = total_over(jnp.sum(kernel, axis=1), "p")
    col_sum = col_total
    for step in range(ROUNDS):
        col_scale = 1.0 / (total * col_sum)
        row_part = jnp.sum(kernel * col_scale[:, None], axis=0)
        if step == 0:
            stats = total_over(jnp.stack([row_part, jnp.sum(kernel, axis=0)]), rows)
            row_sum, row_total = stats[0], stats[1]
        else:
            row_sum = total_over(row_part, rows)
        row_weight = 1.0 / (total * row_sum)
        col_sum = total_over(jnp.sum(kernel * row_weight[None, :], axis=1), "p")
    col_weight = 1.0 - mix_weight + mix_weight * total * col_scale * col_sum
    by_row = 0.5 / row_total
    by_col = 0.5 * col_weight / col_total
    by_pair = mix_weight * total * row_weight
    same = txt_ids[:, None] == img_ids[None, :]
    grad_logit = kernel * (
        by_row[None, :] + by_col[:, None] - by_pair[None, :] * col_scale[:, None]
    ) - jnp.where(same, 1.0 - mix_weight, 0.0)
    grad_logit = grad_logit.astype(jnp.bfloat16)
    g_part = (
        logit_scale * jnp.dot(grad_logit, img_bf, preferred_element_type=jnp.float32)
    ).astype(jnp.bfloat16)
    g_part, grad_logit = lax.optimization_barrier((g_part, grad_logit))
    g_txt = scatter_sum(g_part.reshape(-1, own, width), "p")
    g_part = logit_scale * lax.dot_general(
        grad_logit, txt_bf, (((0,), (0,)), ((), ())), preferred_element_type=jnp.float32
    )
    g_part = keep_half(g_part, "c", 0, jnp.float32)
    g_part = g_part.reshape(NEAR, -1, width)
    g_part = keep_half(g_part, "zh", 1, jnp.bfloat16).astype(jnp.bfloat16)
    g_part, g_txt = lax.optimization_barrier((g_part, g_txt))
    g_img = scatter_sum(g_part.reshape(-1, own, width), ("x", "zl"))
    own_img = lax.dynamic_slice_in_dim(images, t_index * own, own, 0)
    grad_images = project_back(g_img, *normalize(own_img))
    grad_texts = project_back(g_txt, *normalize(texts))
    return (grad_images, grad_texts)


def solution(mesh):
    n_img, n_txt = mesh.devices.shape
    shape = (n_img // CORES, CORES, NEAR, FAR, n_txt // (NEAR * FAR))
    split = Mesh(mesh.devices.reshape(shape), ("p", "c", "x", "zh", "zl"))
    t = ("x", "zh", "zl")
    return jax.shard_map(
        shards,
        mesh=split,
        in_specs=(P(("p", "c"), None), P((*t, "p", "c"), None)),
        out_specs=(P(("p", "c", *t), None), P((*t, "p", "c"), None)),
        check_vma=False,
    )
```

time: 227 us -> 215 us (0.947); the launches traced: 226 us -> 212 us
  waiting for transfers between devices: 62.8 us -> 49.9 us
  matrix products: 6.74 us -> 3.62 us
    all_to_all x4, waiting for transfers between devices: 62.8 us -> 38.2 us  [exchange(): return lax.all_to_all(parts, axes, 0, 0, tiled=True)]
    ppermute x0 -> x2, waiting for transfers between devices: none -> 11.7 us  [keep_half(): lax.ppermute(other.astype(dtype), axis, [(0, 1), (1, 0)])]
    ppermute x0 -> x2, starting transfers between devices: none -> 6.17 us  [keep_half(): lax.ppermute(other.astype(dtype), axis, [(0, 1), (1, 0)])]
    all_to_all x4, starting transfers between devices: 33.2 us -> 28.9 us  [exchange(): return lax.all_to_all(parts, axes, 0, 0, tiled=True)]
    dot_general x3, matrix products: 6.74 us -> 3.62 us  [the longest x1 1.76 us: shards(): jnp.dot(grad_logit, img_bf, preferred_element_type=jnp.float32)]
  transfers between devices with their start and end apart: 4 -> 6, of which waited for: 4 -> 5; matrix products, arithmetic and copies ran while one was open for 2% -> 1% of each run, Pallas kernels for 0% -> 0%
where the time goes in v2:
time: 215 us; the launch traced here: 212 us
  blocking collectives  110 us (51%)
  waiting for transfers between devices  49.9 us (23%)
  starting transfers between devices  35.1 us (16%)
  other arithmetic  8.71 us (4%)
  local copies, waits for them, and re-layouts  3.82 us (2%)
  matrix products  3.62 us (2%)
    all_to_all x6, blocking collectives, exchange(): return lax.all_to_all(parts, axes, 0, 0, tiled=True)  103 us
    all_to_all x4, waiting for transfers between devices, exchange(): return lax.all_to_all(parts, axes, 0, 0, tiled=True)  38.2 us
    all_to_all x4, starting transfers between devices, exchange(): return lax.all_to_all(parts, axes, 0, 0, tiled=True)  28.9 us
    ppermute x2, waiting for transfers between devices, keep_half(): lax.ppermute(other.astype(dtype), axis, [(0, 1), (1, 0)])  11.7 us
    all_gather x1, blocking collectives, shards(): both = lax.all_gather(images, 'c', axis=0, tiled=True)  6.64 us
    ppermute x2, starting transfers between devices, keep_half(): lax.ppermute(other.astype(dtype), axis, [(0, 1), (1, 0)])  6.17 us
  transfers between devices with their start and end apart: 6, of which 5 were waited for; matrix products, arithmetic and copies ran while one was open for 1% of the time, Pallas kernels for 0%

profile of v2, /device:TPU:1, one launch (start us, length us, event | category | flops | bytes accessed | tf_op | source)
XLA Modules:
  0.0 211.7 jit_solution(16446951035386606702)
XLA Ops:
  0.6 1.7 broadcast_in_dim.22
  2.4 13.4 %all-to-all-start = ((bf16[32,24,512]{2,1,0:T(8,128)(2,1)}), bf16[32,24,512]{2,1,0:T(8,128)(2,1)S(1)}, u32[]{:S(2)}, u32[]{:S(2)}) async-start(bf16[32,24,512]{2,1,0:T(8,128)(2,1)} %broadcast_in_dim.22), calls=%async_computation | async-start | bytes 1572864 | tf_op jit(solution)/shard_map/all_to_all | solution.py:28
  15.8 6.6 %all_gather.3 = bf16[768,512]{1,0:T(8,128)(2,1)S(1)} all-gather(bf16[384,512]{1,0:T(8,128)(2,1)S(1)} %copy-done.2), channel_id=1, replica_groups=mesh['p'=32,'c'=2,'x'=2,'zh'=2,'zl'=4] {'c'}, dimensions={0}, use_global_device_ids=true | all-gather | bytes 1179648 | tf_op jit(solution)/shard_map/all_gather | solution.py:58
  22.7 16.7 %all-to-all-done = bf16[32,24,512]{2,1,0:T(8,128)(2,1)S(1)} async-done(((bf16[32,24,512]{2,1,0:T(8,128)(2,1)}), bf16[32,24,512]{2,1,0:T(8,128)(2,1)S(1)}, u32[]{:S(2)}, u32[]{:S(2)}) %all-to-all-start) | async-done | bytes 786464 | tf_op jit(solution)/shard_map/all_to_all | solution.py:28
  40.0 1.1 fusion.19
  41.1 19.4 %all_to_all.56 = f32[32,1,768]{2,1,0:T(1,128)S(1)} all-to-all(f32[32,1,768]{2,1,0:T(1,128)S(1)} %broadcast_in_dim.23), channel_id=1, replica_groups=mesh['p'=32,'c'=2,'x'=2,'zh'=2,'zl'=4] {'p'}, dimensions={0} | all-to-all | bytes 196608 | tf_op jit(solution)/shard_map/all_to_all | solution.py:28
  61.0 28.6 %all_to_all.57 = f32[32,2,768]{2,1,0:T(2,128)S(1)} all-to-all(f32[32,2,768]{2,1,0:T(2,128)S(1)} %broadcast_in_dim.24), channel_id=1, replica_groups=mesh['p'=32,'c'=2,'x'=2,'zh'=2,'zl'=4] {'c','x','zh','zl'}, dimensions={0} | all-to-all | bytes 393216 | tf_op jit(solution)/shard_map/all_to_all | solution.py:28
  90.0 14.5 %all_to_all.58 = f32[32,1,768]{2,1,0:T(1,128)S(1)} all-to-all(f32[32,1,768]{2,1,0:T(1,128)S(1)} %broadcast_in_dim.25), channel_id=1, replica_groups=mesh['p'=32,'c'=2,'x'=2,'zh'=2,'zl'=4] {'p'}, dimensions={0} | all-to-all | bytes 196608 | tf_op jit(solution)/shard_map/all_to_all | solution.py:28
  104.9 13.0 %all_to_all.59 = f32[32,1,768]{2,1,0:T(1,128)S(1)} all-to-all(f32[32,1,768]{2,1,0:T(1,128)S(1)} %broadcast_in_dim.26), channel_id=1, replica_groups=mesh['p'=32,'c'=2,'x'=2,'zh'=2,'zl'=4] {'c','x','zh','zl'}, dimensions={0} | all-to-all | bytes 196608 | tf_op jit(solution)/shard_map/all_to_all | solution.py:28
  118.3 14.4 %all_to_all.60 = f32[32,1,768]{2,1,0:T(1,128)S(1)} all-to-all(f32[32,1,768]{2,1,0:T(1,128)S(1)} %broadcast_in_dim.27), channel_id=1, replica_groups=mesh['p'=32,'c'=2,'x'=2,'zh'=2,'zl'=4] {'p'}, dimensions={0} | all-to-all | bytes 196608 | tf_op jit(solution)/shard_map/all_to_all | solution.py:28
  133.1 12.9 %all_to_all.61 = f32[32,1,768]{2,1,0:T(1,128)S(1)} all-to-all(f32[32,1,768]{2,1,0:T(1,128)S(1)} %broadcast_in_dim.28), channel_id=1, replica_groups=mesh['p'=32,'c'=2,'x'=2,'zh'=2,'zl'=4] {'c','x','zh','zl'}, dimensions={0} | all-to-all | bytes 196608 | tf_op jit(solution)/shard_map/all_to_all | solution.py:28
  147.0 3.9 %all-to-all-start.7 = ((f32[32,1,768]{2,1,0:T(1,128)}), f32[32,1,768]{2,1,0:T(1,128)S(1)}, u32[]{:S(2)}, u32[]{:S(2)}) async-start(f32[32,1,768]{2,1,0:T(1,128)} %broadcast_in_dim.29), calls=%async_computation.7 | async-start | bytes 196608 | tf_op jit(solution)/shard_map/all_to_all | solution.py:28
  150.9 11.4 %all-to-all-done.7 = f32[32,1,768]{2,1,0:T(1,128)S(1)} async-done(((f32[32,1,768]{2,1,0:T(1,128)}), f32[32,1,768]{2,1,0:T(1,128)S(1)}, u32[]{:S(2)}, u32[]{:S(2)}) %all-to-all-start.7) | async-done | bytes 98336 | tf_op jit(solution)/shard_map/all_to_all | solution.py:28
  163.1 1.8 multiply_convert_fusion
  165.7 1.0 constant_dynamic-slice_fusion
  166.6 3.8 %collective-permute-start = (f32[384,512]{1,0:T(8,128)}, f32[384,512]{1,0:T(8,128)S(1)}, u32[]{:S(2)}, u32[]{:S(2)}) collective-permute-start(f32[384,512]{1,0:T(8,128)} %constant_dynamic-slice_fusion), channel_id=1, source_target_pairs={{0,16},{16,0},{1,17},{17,1},{2,18},{18,2},{3,19},{19,3},{4,20},{20... | collective-permute-start | bytes 2359304 | tf_op jit(solution)/shard_map/ppermute | solution.py:48
  170.4 3.9 %all-to-all-start.8 = ((bf16[32,24,512]{2,1,0:T(8,128)(2,1)}), bf16[32,24,512]{2,1,0:T(8,128)(2,1)S(1)}, u32[]{:S(2)}, u32[]{:S(2)}) async-start(bf16[32,24,512]{2,1,0:T(8,128)(2,1)} %bitcast.13), calls=%async_computation.8 | async-start | bytes 1572864 | tf_op jit(solution)/shard_map/all_to_all | solution.py:28
  175.5 2.4 %collective-permute-start.1 = (bf16[2,96,512]{2,1,0:T(8,128)(2,1)S(1)}, bf16[2,96,512]{2,1,0:T(8,128)(2,1)S(1)}, u32[]{:S(2)}, u32[]{:S(2)}) collective-permute-start(bf16[2,96,512]{2,1,0:T(8,128)(2,1)S(1)} %dynamic-slice_convert_fusion), channel_id=1, source_target_pairs={{0,4},{4,0},{1,5},{5,1},{2,6},{6,2},{3,7},{7,3},{8,12},{12,8},{9,1... | collective-permute-start | bytes 589832 | tf_op jit(solution)/shard_map/ppermute | solution.py:48
  178.0 11.7 %collective-permute-done.1 = bf16[2,96,512]{2,1,0:T(8,128)(2,1)S(1)} collective-permute-done((bf16[2,96,512]{2,1,0:T(8,128)(2,1)S(1)}, bf16[2,96,512]{2,1,0:T(8,128)(2,1)S(1)}, u32[]{:S(2)}, u32[]{:S(2)}) %collective-permute-start.1) | collective-permute-done | bytes 196640 | tf_op jit(solution)/shard_map/ppermute | solution.py:48
  190.4 4.7 %all-to-all-done.8 = bf16[32,24,512]{2,1,0:T(8,128)(2,1)S(1)} async-done(((bf16[32,24,512]{2,1,0:T(8,128)(2,1)}), bf16[32,24,512]{2,1,0:T(8,128)(2,1)S(1)}, u32[]{:S(2)}, u32[]{:S(2)}) %all-to-all-start.8) | async-done | bytes 786464 | tf_op jit(solution)/shard_map/all_to_all | solution.py:28
  195.3 7.7 %all-to-all-start.9 = ((bf16[8,24,512]{2,1,0:T(8,128)(2,1)}), bf16[8,24,512]{2,1,0:T(8,128)(2,1)S(1)}, u32[]{:S(2)}, u32[]{:S(2)}) async-start(bf16[8,24,512]{2,1,0:T(8,128)(2,1)} %bitcast.3), calls=%async_computation.9 | async-start | bytes 393216 | tf_op jit(solution)/shard_map/all_to_all | solution.py:28
  203.9 5.4 %all-to-all-done.9 = bf16[8,24,512]{2,1,0:T(8,128)(2,1)S(1)} async-done(((bf16[8,24,512]{2,1,0:T(8,128)(2,1)}), bf16[8,24,512]{2,1,0:T(8,128)(2,1)S(1)}, u32[]{:S(2)}, u32[]{:S(2)}) %all-to-all-start.9) | async-done | bytes 196640 | tf_op jit(solution)/shard_map/all_to_all | solution.py:28
  209.3 0.9 multiply_reduce_fusion.8
  210.2 1.4 subtract_divide_fusion.1
  (59 shorter events, 8.3 us)
Async XLA Ops:
  0.6 15.2 %copy-start.2 = (bf16[384,512]{1,0:T(8,128)(2,1)S(1)}, bf16[384,512]{1,0:T(8,128)(2,1)}, u32[]{:S(2)}) copy-start(bf16[384,512]{1,0:T(8,128)(2,1)} %param.2) | copy-start | bytes 1179652
  2.4 37.0 %all-to-all-start = ((bf16[32,24,512]{2,1,0:T(8,128)(2,1)}), bf16[32,24,512]{2,1,0:T(8,128)(2,1)S(1)}, u32[]{:S(2)}, u32[]{:S(2)}) async-start(bf16[32,24,512]{2,1,0:T(8,128)(2,1)} %broadcast_in_dim.22), calls=%async_computation | async-start | bytes 1572864 | tf_op jit(solution)/shard_map/all_to_all | solution.py:28
  39.9 1.1 copy-start
  147.0 15.3 %all-to-all-start.7 = ((f32[32,1,768]{2,1,0:T(1,128)}), f32[32,1,768]{2,1,0:T(1,128)S(1)}, u32[]{:S(2)}, u32[]{:S(2)}) async-start(f32[32,1,768]{2,1,0:T(1,128)} %broadcast_in_dim.29), calls=%async_computation.7 | async-start | bytes 196608 | tf_op jit(solution)/shard_map/all_to_all | solution.py:28
  163.1 1.8 copy-start.1
  165.7 9.5 %copy-start.3 = (bf16[24,512]{1,0:T(8,128)(2,1)S(1)}, bf16[24,512]{1,0:T(8,128)(2,1)}, u32[]{:S(2)}) copy-start(bf16[24,512]{1,0:T(8,128)(2,1)} %param.3) | copy-start | bytes 73732
  166.6 8.7 %collective-permute-start = (f32[384,512]{1,0:T(8,128)}, f32[384,512]{1,0:T(8,128)S(1)}, u32[]{:S(2)}, u32[]{:S(2)}) collective-permute-start(f32[384,512]{1,0:T(8,128)} %constant_dynamic-slice_fusion), channel_id=1, source_target_pairs={{0,16},{16,0},{1,17},{17,1},{2,18},{18,2},{3,19},{19,3},{4,20},{20... | collective-permute-start | bytes 2359304 | tf_op jit(solution)/shard_map/ppermute | solution.py:48
  170.4 24.7 %all-to-all-start.8 = ((bf16[32,24,512]{2,1,0:T(8,128)(2,1)}), bf16[32,24,512]{2,1,0:T(8,128)(2,1)S(1)}, u32[]{:S(2)}, u32[]{:S(2)}) async-start(bf16[32,24,512]{2,1,0:T(8,128)(2,1)} %bitcast.13), calls=%async_computation.8 | async-start | bytes 1572864 | tf_op jit(solution)/shard_map/all_to_all | solution.py:28
  175.5 14.2 %collective-permute-start.1 = (bf16[2,96,512]{2,1,0:T(8,128)(2,1)S(1)}, bf16[2,96,512]{2,1,0:T(8,128)(2,1)S(1)}, u32[]{:S(2)}, u32[]{:S(2)}) collective-permute-start(bf16[2,96,512]{2,1,0:T(8,128)(2,1)S(1)} %dynamic-slice_convert_fusion), channel_id=1, source_target_pairs={{0,4},{4,0},{1,5},{5,1},{2,6},{6,2},{3,7},{7,3},{8,12},{12,8},{9,1... | collective-permute-start | bytes 589832 | tf_op jit(solution)/shard_map/ppermute | solution.py:48
  195.3 14.0 %all-to-all-start.9 = ((bf16[8,24,512]{2,1,0:T(8,128)(2,1)}), bf16[8,24,512]{2,1,0:T(8,128)(2,1)S(1)}, u32[]{:S(2)}, u32[]{:S(2)}) async-start(bf16[8,24,512]{2,1,0:T(8,128)(2,1)} %bitcast.3), calls=%async_computation.9 | async-start | bytes 393216 | tf_op jit(solution)/shard_map/all_to_all | solution.py:28

commit v3 on v2

--- a/solution.py
+++ b/solution.py
@@ -40,12 +40,19 @@
     return jnp.sum(exchange(values.astype(jnp.bfloat16), axes).astype(jnp.float32), axis=0)
 
 
-def keep_half(values, axis, dim, dtype):
-    me = lax.axis_index(axis)
+def keep_half(values, start, axis, dim):
     half = values.shape[dim] // 2
-    mine = lax.dynamic_slice_in_dim(values, me * half, half, dim)
-    other = lax.dynamic_slice_in_dim(values, (1 - me) * half, half, dim)
-    return mine + lax.ppermute(other.astype(dtype), axis, [(0, 1), (1, 0)]).astype(jnp.float32)
+    mine = take(values, start[0], half, dim)
+    other = take(values, start[1], half, dim).astype(jnp.bfloat16)
+    return mine + lax.ppermute(other, axis, [(0, 1), (1, 0)]).astype(jnp.float32)
+
+
+def take(values, start, size, dim):
+    starts = [jnp.uint32(0)] * values.ndim
+    starts[dim] = start
+    sizes = list(values.shape)
+    sizes[dim] = size
+    return lax.dynamic_slice(values, starts, sizes)
 
 
 def shards(images, texts):
@@ -61,7 +68,15 @@
     img_ids = p_index * n_img + jnp.arange(n_img, dtype=jnp.int32)
     place = jnp.arange(n_txt, dtype=jnp.int32)
     txt_ids = t_index * (n_txt * CORES) + (place // own * CORES + c_index) * own + place % own
-    both, img_ids, txt_ids = lax.optimization_barrier((both, img_ids, txt_ids))
+    half_c, half_z = n_img // 2, n_img // (2 * NEAR * FAR)
+    z_index = lax.axis_index("zh")
+    places = [c_index * half_c, (1 - c_index) * half_c, z_index * half_z, (1 - z_index) * half_z]
+    places = [place.astype(jnp.uint32) for place in places]
+    own_img = lax.dynamic_slice_in_dim(images, t_index * own, own, 0)
+    own_units = normalize(own_img) + normalize(texts)
+    both, img_ids, txt_ids, places, own_units = lax.optimization_barrier(
+        (both, img_ids, txt_ids, places, own_units)
+    )
     img_bf = normalize(both)[0].astype(jnp.bfloat16)
     txt_bf = normalize(raw_txt)[0].astype(jnp.bfloat16)
     scores = logit_scale * lax.dot_general(
@@ -97,14 +112,13 @@
     g_part = logit_scale * lax.dot_general(
         grad_logit, txt_bf, (((0,), (0,)), ((), ())), preferred_element_type=jnp.float32
     )
-    g_part = keep_half(g_part, "c", 0, jnp.float32)
+    g_part = keep_half(g_part, places[:2], "c", 0)
     g_part = g_part.reshape(NEAR, -1, width)
-    g_part = keep_half(g_part, "zh", 1, jnp.bfloat16).astype(jnp.bfloat16)
+    g_part = keep_half(g_part, places[2:], "zh", 1).astype(jnp.bfloat16)
     g_part, g_txt = lax.optimization_barrier((g_part, g_txt))
     g_img = scatter_sum(g_part.reshape(-1, own, width), ("x", "zl"))
-    own_img = lax.dynamic_slice_in_dim(images, t_index * own, own, 0)
-    grad_images = project_back(g_img, *normalize(own_img))
-    grad_texts = project_back(g_txt, *normalize(texts))
+    grad_images = project_back(g_img, *own_units[:2])
+    grad_texts = project_back(g_txt, *own_units[2:])
     return (grad_images, grad_texts)
 
 

time: 215 us -> 206 us (0.958)
  waiting for transfers between devices: 49.9 us -> 34.3 us
  blocking collectives: 110 us -> 124 us
  starting transfers between devices: 35.1 us -> 30.7 us
  other arithmetic: 8.71 us -> 6.49 us
    all_to_all x4 -> x3, waiting for transfers between devices: 38.2 us -> 21.6 us  [exchange(): return lax.all_to_all(parts, axes, 0, 0, tiled=True)]
    all_to_all x6 -> x7, blocking collectives: 103 us -> 117 us  [exchange(): return lax.all_to_all(parts, axes, 0, 0, tiled=True)]
    all_to_all x4 -> x3, starting transfers between devices: 28.9 us -> 24.5 us  [exchange(): return lax.all_to_all(parts, axes, 0, 0, tiled=True)]
  transfers between devices with their start and end apart: 6 -> 5, of which waited for: 5 -> 4; matrix products, arithmetic and copies ran while one was open for 1% -> 2% of each run, Pallas kernels for 0% -> 0%
where the time goes in v3:
time: 206 us; the launch traced here: 204 us
  blocking collectives  124 us (60%)
  waiting for transfers between devices  34.3 us (17%)
  starting transfers between devices  30.7 us (15%)
  other arithmetic  6.49 us (3%)
  matrix products  4.93 us (2%)
  local copies, waits for them, and re-layouts  2.35 us (1%)
    all_to_all x7, blocking collectives, exchange(): return lax.all_to_all(parts, axes, 0, 0, tiled=True)  117 us
    all_to_all x3, starting transfers between devices, exchange(): return lax.all_to_all(parts, axes, 0, 0, tiled=True)  24.5 us
    all_to_all x3, waiting for transfers between devices, exchange(): return lax.all_to_all(parts, axes, 0, 0, tiled=True)  21.6 us
    ppermute x2, waiting for transfers between devices, keep_half(): lax.ppermute(other, axis, [(0, 1), (1, 0)]).astype(jnp.float32)  12.7 us
    all_gather x1, blocking collectives, shards(): both = lax.all_gather(images, 'c', axis=0, tiled=True)  6.64 us
    ppermute x2, starting transfers between devices, keep_half(): lax.ppermute(other, axis, [(0, 1), (1, 0)]).astype(jnp.float32)  6.18 us
  transfers between devices with their start and end apart: 5, of which 4 were waited for; matrix products, arithmetic and copies ran while one was open for 2% of the time, Pallas kernels for 0%

profile of v3, /device:TPU:1, one launch (start us, length us, event | category | flops | bytes accessed | tf_op | source)
XLA Modules:
  0.0 203.7 jit_solution(17311850476441978932)
XLA Ops:
  0.6 1.7 broadcast_in_dim.22
  2.4 13.4 %all-to-all-start = ((bf16[32,24,512]{2,1,0:T(8,128)(2,1)}), bf16[32,24,512]{2,1,0:T(8,128)(2,1)S(1)}, u32[]{:S(2)}, u32[]{:S(2)}) async-start(bf16[32,24,512]{2,1,0:T(8,128)(2,1)} %broadcast_in_dim.22), calls=%async_computation | async-start | bytes 1572864 | tf_op jit(solution)/shard_map/all_to_all | solution.py:28
  16.1 6.6 %all_gather.3 = bf16[768,512]{1,0:T(8,128)(2,1)S(1)} all-gather(bf16[384,512]{1,0:T(8,128)(2,1)S(1)} %copy-done.3), channel_id=1, replica_groups=mesh['p'=32,'c'=2,'x'=2,'zh'=2,'zl'=4] {'c'}, dimensions={0}, use_global_device_ids=true | all-gather | bytes 1179648 | tf_op jit(solution)/shard_map/all_gather | solution.py:65
  23.1 16.2 %all-to-all-done = bf16[32,24,512]{2,1,0:T(8,128)(2,1)S(1)} async-done(((bf16[32,24,512]{2,1,0:T(8,128)(2,1)}), bf16[32,24,512]{2,1,0:T(8,128)(2,1)S(1)}, u32[]{:S(2)}, u32[]{:S(2)}) %all-to-all-start) | async-done | bytes 786464 | tf_op jit(solution)/shard_map/all_to_all | solution.py:28
  40.0 1.1 fusion.21
  41.1 19.4 %all_to_all.56 = f32[32,1,768]{2,1,0:T(1,128)S(1)} all-to-all(f32[32,1,768]{2,1,0:T(1,128)S(1)} %broadcast_in_dim.23), channel_id=1, replica_groups=mesh['p'=32,'c'=2,'x'=2,'zh'=2,'zl'=4] {'p'}, dimensions={0} | all-to-all | bytes 196608 | tf_op jit(solution)/shard_map/all_to_all | solution.py:28
  61.0 28.6 %all_to_all.57 = f32[32,2,768]{2,1,0:T(2,128)S(1)} all-to-all(f32[32,2,768]{2,1,0:T(2,128)S(1)} %broadcast_in_dim.24), channel_id=1, replica_groups=mesh['p'=32,'c'=2,'x'=2,'zh'=2,'zl'=4] {'c','x','zh','zl'}, dimensions={0} | all-to-all | bytes 393216 | tf_op jit(solution)/shard_map/all_to_all | solution.py:28
  90.0 14.5 %all_to_all.58 = f32[32,1,768]{2,1,0:T(1,128)S(1)} all-to-all(f32[32,1,768]{2,1,0:T(1,128)S(1)} %broadcast_in_dim.25), channel_id=1, replica_groups=mesh['p'=32,'c'=2,'x'=2,'zh'=2,'zl'=4] {'p'}, dimensions={0} | all-to-all | bytes 196608 | tf_op jit(solution)/shard_map/all_to_all | solution.py:28
  104.9 13.0 %all_to_all.59 = f32[32,1,768]{2,1,0:T(1,128)S(1)} all-to-all(f32[32,1,768]{2,1,0:T(1,128)S(1)} %broadcast_in_dim.26), channel_id=1, replica_groups=mesh['p'=32,'c'=2,'x'=2,'zh'=2,'zl'=4] {'c','x','zh','zl'}, dimensions={0} | all-to-all | bytes 196608 | tf_op jit(solution)/shard_map/all_to_all | solution.py:28
  118.3 14.4 %all_to_all.60 = f32[32,1,768]{2,1,0:T(1,128)S(1)} all-to-all(f32[32,1,768]{2,1,0:T(1,128)S(1)} %broadcast_in_dim.27), channel_id=1, replica_groups=mesh['p'=32,'c'=2,'x'=2,'zh'=2,'zl'=4] {'p'}, dimensions={0} | all-to-all | bytes 196608 | tf_op jit(solution)/shard_map/all_to_all | solution.py:28
  133.1 12.9 %all_to_all.61 = f32[32,1,768]{2,1,0:T(1,128)S(1)} all-to-all(f32[32,1,768]{2,1,0:T(1,128)S(1)} %broadcast_in_dim.28), channel_id=1, replica_groups=mesh['p'=32,'c'=2,'x'=2,'zh'=2,'zl'=4] {'c','x','zh','zl'}, dimensions={0} | all-to-all | bytes 196608 | tf_op jit(solution)/shard_map/all_to_all | solution.py:28
  146.4 14.4 %all_to_all.62 = f32[32,1,768]{2,1,0:T(1,128)S(1)} all-to-all(f32[32,1,768]{2,1,0:T(1,128)S(1)} %broadcast_in_dim.29), channel_id=1, replica_groups=mesh['p'=32,'c'=2,'x'=2,'zh'=2,'zl'=4] {'p'}, dimensions={0} | all-to-all | bytes 196608 | tf_op jit(solution)/shard_map/all_to_all | solution.py:28
  161.6 1.8 multiply_convert_fusion
  163.4 3.9 %all-to-all-start.8 = ((bf16[32,24,512]{2,1,0:T(8,128)(2,1)}), bf16[32,24,512]{2,1,0:T(8,128)(2,1)S(1)}, u32[]{:S(2)}, u32[]{:S(2)}) async-start(bf16[32,24,512]{2,1,0:T(8,128)(2,1)} %bitcast.4), calls=%async_computation.8 | async-start | bytes 1572864 | tf_op jit(solution)/shard_map/all_to_all | solution.py:28
  167.3 2.1 %convolution_multiply_fusion = f32[768,512]{1,0:T(8,128)S(1)} fusion(bf16[768,768]{1,0:T(8,128)(2,1)} %copy-done, bf16[768,512]{1,0:T(8,128)(2,1)S(1)} %copy-done.2), kind=kOutput, calls=%fused_computation.17 | convolution fusion | flops 604372992 | bytes 3538944 | tf_op jit(solution)/shard_map/dot_general | solution.py:112
  169.5 3.8 %collective-permute-start = (bf16[384,512]{1,0:T(8,128)(2,1)S(1)}, bf16[384,512]{1,0:T(8,128)(2,1)S(1)}, u32[]{:S(2)}, u32[]{:S(2)}) collective-permute-start(bf16[384,512]{1,0:T(8,128)(2,1)S(1)} %dynamic-slice_convert_fusion), channel_id=1, source_target_pairs={{0,16},{16,0},{1,17},{17,1},{2,18},{18,2},{3,19},{19,3},{4,20},{20... | collective-permute-start | bytes 1179656 | tf_op jit(solution)/shard_map/ppermute | solution.py:47
  173.3 1.3 collective-permute-done
  174.8 2.4 %collective-permute-start.1 = (bf16[2,96,512]{2,1,0:T(8,128)(2,1)S(1)}, bf16[2,96,512]{2,1,0:T(8,128)(2,1)S(1)}, u32[]{:S(2)}, u32[]{:S(2)}) collective-permute-start(bf16[2,96,512]{2,1,0:T(8,128)(2,1)S(1)} %dynamic-slice_convert_fusion.1), channel_id=1, source_target_pairs={{0,4},{4,0},{1,5},{5,1},{2,6},{6,2},{3,7},{7,3},{8,12},{12,8},{9,1... | collective-permute-start | bytes 589832 | tf_op jit(solution)/shard_map/ppermute | solution.py:47
  177.2 11.4 %collective-permute-done.1 = bf16[2,96,512]{2,1,0:T(8,128)(2,1)S(1)} collective-permute-done((bf16[2,96,512]{2,1,0:T(8,128)(2,1)S(1)}, bf16[2,96,512]{2,1,0:T(8,128)(2,1)S(1)}, u32[]{:S(2)}, u32[]{:S(2)}) %collective-permute-start.1) | collective-permute-done | bytes 196640 | tf_op jit(solution)/shard_map/ppermute | solution.py:47
  188.6 0.7 add_convert_fusion
  189.5 7.2 %all-to-all-start.9 = ((bf16[8,24,512]{2,1,0:T(8,128)(2,1)}), bf16[8,24,512]{2,1,0:T(8,128)(2,1)S(1)}, u32[]{:S(2)}, u32[]{:S(2)}) async-start(bf16[8,24,512]{2,1,0:T(8,128)(2,1)} %bitcast.5), calls=%async_computation.9 | async-start | bytes 393216 | tf_op jit(solution)/shard_map/all_to_all | solution.py:28
  196.8 0.7 subtract_divide_fusion
  197.5 5.4 %all-to-all-done.9 = bf16[8,24,512]{2,1,0:T(8,128)(2,1)S(1)} async-done(((bf16[8,24,512]{2,1,0:T(8,128)(2,1)}), bf16[8,24,512]{2,1,0:T(8,128)(2,1)S(1)}, u32[]{:S(2)}, u32[]{:S(2)}) %all-to-all-start.9) | async-done | bytes 196640 | tf_op jit(solution)/shard_map/all_to_all | solution.py:28
  203.0 0.7 subtract_divide_fusion.1
  (62 shorter events, 5.0 us)
Async XLA Ops:
  0.6 15.2 %copy-start.4 = (bf16[24,512]{1,0:T(8,128)(2,1)S(1)}, bf16[24,512]{1,0:T(8,128)(2,1)}, u32[]{:S(2)}) copy-start(bf16[24,512]{1,0:T(8,128)(2,1)} %param.3) | copy-start | bytes 73732
  0.6 15.3 %copy-start.3 = (bf16[384,512]{1,0:T(8,128)(2,1)S(1)}, bf16[384,512]{1,0:T(8,128)(2,1)}, u32[]{:S(2)}) copy-start(bf16[384,512]{1,0:T(8,128)(2,1)} %param.2) | copy-start | bytes 1179652
  2.4 37.0 %all-to-all-start = ((bf16[32,24,512]{2,1,0:T(8,128)(2,1)}), bf16[32,24,512]{2,1,0:T(8,128)(2,1)S(1)}, u32[]{:S(2)}, u32[]{:S(2)}) async-start(bf16[32,24,512]{2,1,0:T(8,128)(2,1)} %broadcast_in_dim.22), calls=%async_computation | async-start | bytes 1572864 | tf_op jit(solution)/shard_map/all_to_all | solution.py:28
  40.0 1.1 copy-start.1
  161.6 1.8 copy-start
  161.6 5.7 %copy-start.2 = (bf16[768,512]{1,0:T(8,128)(2,1)S(1)}, bf16[768,512]{1,0:T(8,128)(2,1)}, u32[]{:S(2)}) copy-start(bf16[768,512]{1,0:T(8,128)(2,1)} %copy-done.1) | copy-start | bytes 2359300
  163.4 25.9 %all-to-all-start.8 = ((bf16[32,24,512]{2,1,0:T(8,128)(2,1)}), bf16[32,24,512]{2,1,0:T(8,128)(2,1)S(1)}, u32[]{:S(2)}, u32[]{:S(2)}) async-start(bf16[32,24,512]{2,1,0:T(8,128)(2,1)} %bitcast.4), calls=%async_computation.8 | async-start | bytes 1572864 | tf_op jit(solution)/shard_map/all_to_all | solution.py:28
  169.5 5.1 %collective-permute-start = (bf16[384,512]{1,0:T(8,128)(2,1)S(1)}, bf16[384,512]{1,0:T(8,128)(2,1)S(1)}, u32[]{:S(2)}, u32[]{:S(2)}) collective-permute-start(bf16[384,512]{1,0:T(8,128)(2,1)S(1)} %dynamic-slice_convert_fusion), channel_id=1, source_target_pairs={{0,16},{16,0},{1,17},{17,1},{2,18},{18,2},{3,19},{19,3},{4,20},{20... | collective-permute-start | bytes 1179656 | tf_op jit(solution)/shard_map/ppermute | solution.py:47
  174.8 13.8 %collective-permute-start.1 = (bf16[2,96,512]{2,1,0:T(8,128)(2,1)S(1)}, bf16[2,96,512]{2,1,0:T(8,128)(2,1)S(1)}, u32[]{:S(2)}, u32[]{:S(2)}) collective-permute-start(bf16[2,96,512]{2,1,0:T(8,128)(2,1)S(1)} %dynamic-slice_convert_fusion.1), channel_id=1, source_target_pairs={{0,4},{4,0},{1,5},{5,1},{2,6},{6,2},{3,7},{7,3},{8,12},{12,8},{9,1... | collective-permute-start | bytes 589832 | tf_op jit(solution)/shard_map/ppermute | solution.py:47
  189.5 13.4 %all-to-all-start.9 = ((bf16[8,24,512]{2,1,0:T(8,128)(2,1)}), bf16[8,24,512]{2,1,0:T(8,128)(2,1)S(1)}, u32[]{:S(2)}, u32[]{:S(2)}) async-start(bf16[8,24,512]{2,1,0:T(8,128)(2,1)} %bitcast.5), calls=%async_computation.9 | async-start | bytes 393216 | tf_op jit(solution)/shard_map/all_to_all | solution.py:28

commit v4 on v3

--- a/solution.py
+++ b/solution.py
@@ -100,23 +100,24 @@
     by_col = 0.5 * col_weight / col_total
     by_pair = mix_weight * total * row_weight
     same = txt_ids[:, None] == img_ids[None, :]
-    grad_logit = kernel * (
-        by_row[None, :] + by_col[:, None] - by_pair[None, :] * col_scale[:, None]
-    ) - jnp.where(same, 1.0 - mix_weight, 0.0)
-    grad_logit = grad_logit.astype(jnp.bfloat16)
-    g_part = (
-        logit_scale * jnp.dot(grad_logit, img_bf, preferred_element_type=jnp.float32)
-    ).astype(jnp.bfloat16)
-    g_part, grad_logit = lax.optimization_barrier((g_part, grad_logit))
-    g_txt = scatter_sum(g_part.reshape(-1, own, width), "p")
-    g_part = logit_scale * lax.dot_general(
-        grad_logit, txt_bf, (((0,), (0,)), ((), ())), preferred_element_type=jnp.float32
+
+    def logits(kernel):
+        grad_logit = kernel * (
+            by_row[None, :] + by_col[:, None] - by_pair[None, :] * col_scale[:, None]
+        ) - jnp.where(same, 1.0 - mix_weight, 0.0)
+        return grad_logit.astype(jnp.bfloat16)
+
+    g_part = jnp.dot(logits(kernel), img_bf, preferred_element_type=jnp.float32)
+    g_part, kernel = lax.optimization_barrier((g_part.astype(jnp.bfloat16), kernel))
+    g_txt = logit_scale * scatter_sum(g_part.reshape(-1, own, width), "p")
+    g_part = lax.dot_general(
+        logits(kernel), txt_bf, (((0,), (0,)), ((), ())), preferred_element_type=jnp.float32
     )
     g_part = keep_half(g_part, places[:2], "c", 0)
     g_part = g_part.reshape(NEAR, -1, width)
     g_part = keep_half(g_part, places[2:], "zh", 1).astype(jnp.bfloat16)
     g_part, g_txt = lax.optimization_barrier((g_part, g_txt))
-    g_img = scatter_sum(g_part.reshape(-1, own, width), ("x", "zl"))
+    g_img = logit_scale * scatter_sum(g_part.reshape(-1, own, width), ("x", "zl"))
     grad_images = project_back(g_img, *own_units[:2])
     grad_texts = project_back(g_txt, *own_units[2:])
     return (grad_images, grad_texts)

time: 206 us -> 205 us (level)
  no operation moved by 1% of the time
where the time goes in v4:
time: 205 us; the launch traced here: 203 us
  blocking collectives  124 us (60%)
  waiting for transfers between devices  34.3 us (17%)
  starting transfers between devices  30.4 us (15%)
  other arithmetic  5.87 us (3%)
  matrix products  5.29 us (3%)
  local copies, waits for them, and re-layouts  2.34 us (1%)
    all_to_all x7, blocking collectives, exchange(): return lax.all_to_all(parts, axes, 0, 0, tiled=True)  117 us
    all_to_all x3, starting transfers between devices, exchange(): return lax.all_to_all(parts, axes, 0, 0, tiled=True)  24.2 us
    all_to_all x3, waiting for transfers between devices, exchange(): return lax.all_to_all(parts, axes, 0, 0, tiled=True)  21.6 us
    ppermute x2, waiting for transfers between devices, keep_half(): lax.ppermute(other, axis, [(0, 1), (1, 0)]).astype(jnp.float32)  12.7 us
    all_gather x1, blocking collectives, shards(): both = lax.all_gather(images, 'c', axis=0, tiled=True)  6.64 us
    ppermute x2, starting transfers between devices, keep_half(): lax.ppermute(other, axis, [(0, 1), (1, 0)]).astype(jnp.float32)  6.19 us
  transfers between devices with their start and end apart: 5, of which 4 were waited for; matrix products, arithmetic and copies ran while one was open for 2% of the time, Pallas kernels for 0%

profile of v4, /device:TPU:1, one launch (start us, length us, event | category | flops | bytes accessed | tf_op | source)
XLA Modules:
  0.0 203.1 jit_solution(10403290533088586390)
XLA Ops:
  0.6 1.7 broadcast_in_dim.24
  2.4 13.4 %all-to-all-start = ((bf16[32,24,512]{2,1,0:T(8,128)(2,1)}), bf16[32,24,512]{2,1,0:T(8,128)(2,1)S(1)}, u32[]{:S(2)}, u32[]{:S(2)}) async-start(bf16[32,24,512]{2,1,0:T(8,128)(2,1)} %broadcast_in_dim.24), calls=%async_computation | async-start | bytes 1572864 | tf_op jit(solution)/shard_map/all_to_all | solution.py:28
  16.1 6.6 %all_gather.3 = bf16[768,512]{1,0:T(8,128)(2,1)S(1)} all-gather(bf16[384,512]{1,0:T(8,128)(2,1)S(1)} %copy-done.1), channel_id=1, replica_groups=mesh['p'=32,'c'=2,'x'=2,'zh'=2,'zl'=4] {'c'}, dimensions={0}, use_global_device_ids=true | all-gather | bytes 1179648 | tf_op jit(solution)/shard_map/all_gather | solution.py:65
  23.1 16.2 %all-to-all-done = bf16[32,24,512]{2,1,0:T(8,128)(2,1)S(1)} async-done(((bf16[32,24,512]{2,1,0:T(8,128)(2,1)}), bf16[32,24,512]{2,1,0:T(8,128)(2,1)S(1)}, u32[]{:S(2)}, u32[]{:S(2)}) %all-to-all-start) | async-done | bytes 786464 | tf_op jit(solution)/shard_map/all_to_all | solution.py:28
  40.0 1.1 fusion.46
  41.1 19.4 %all_to_all.56 = f32[32,1,768]{2,1,0:T(1,128)S(1)} all-to-all(f32[32,1,768]{2,1,0:T(1,128)S(1)} %broadcast_in_dim.25), channel_id=1, replica_groups=mesh['p'=32,'c'=2,'x'=2,'zh'=2,'zl'=4] {'p'}, dimensions={0} | all-to-all | bytes 196608 | tf_op jit(solution)/shard_map/all_to_all | solution.py:28
  61.0 28.6 %all_to_all.57 = f32[32,2,768]{2,1,0:T(2,128)S(1)} all-to-all(f32[32,2,768]{2,1,0:T(2,128)S(1)} %broadcast_in_dim.26), channel_id=1, replica_groups=mesh['p'=32,'c'=2,'x'=2,'zh'=2,'zl'=4] {'c','x','zh','zl'}, dimensions={0} | all-to-all | bytes 393216 | tf_op jit(solution)/shard_map/all_to_all | solution.py:28
  90.0 14.5 %all_to_all.58 = f32[32,1,768]{2,1,0:T(1,128)S(1)} all-to-all(f32[32,1,768]{2,1,0:T(1,128)S(1)} %broadcast_in_dim.27), channel_id=1, replica_groups=mesh['p'=32,'c'=2,'x'=2,'zh'=2,'zl'=4] {'p'}, dimensions={0} | all-to-all | bytes 196608 | tf_op jit(solution)/shard_map/all_to_all | solution.py:28
  104.9 13.0 %all_to_all.59 = f32[32,1,768]{2,1,0:T(1,128)S(1)} all-to-all(f32[32,1,768]{2,1,0:T(1,128)S(1)} %broadcast_in_dim.28), channel_id=1, replica_groups=mesh['p'=32,'c'=2,'x'=2,'zh'=2,'zl'=4] {'c','x','zh','zl'}, dimensions={0} | all-to-all | bytes 196608 | tf_op jit(solution)/shard_map/all_to_all | solution.py:28
  118.3 14.4 %all_to_all.60 = f32[32,1,768]{2,1,0:T(1,128)S(1)} all-to-all(f32[32,1,768]{2,1,0:T(1,128)S(1)} %broadcast_in_dim.29), channel_id=1, replica_groups=mesh['p'=32,'c'=2,'x'=2,'zh'=2,'zl'=4] {'p'}, dimensions={0} | all-to-all | bytes 196608 | tf_op jit(solution)/shard_map/all_to_all | solution.py:28
  133.1 12.9 %all_to_all.61 = f32[32,1,768]{2,1,0:T(1,128)S(1)} all-to-all(f32[32,1,768]{2,1,0:T(1,128)S(1)} %broadcast_in_dim.30), channel_id=1, replica_groups=mesh['p'=32,'c'=2,'x'=2,'zh'=2,'zl'=4] {'c','x','zh','zl'}, dimensions={0} | all-to-all | bytes 196608 | tf_op jit(solution)/shard_map/all_to_all | solution.py:28
  146.4 14.4 %all_to_all.62 = f32[32,1,768]{2,1,0:T(1,128)S(1)} all-to-all(f32[32,1,768]{2,1,0:T(1,128)S(1)} %broadcast_in_dim.31), channel_id=1, replica_groups=mesh['p'=32,'c'=2,'x'=2,'zh'=2,'zl'=4] {'p'}, dimensions={0} | all-to-all | bytes 196608 | tf_op jit(solution)/shard_map/all_to_all | solution.py:28
  160.9 1.9 convolution_convert_fusion
  162.9 3.9 %all-to-all-start.8 = ((bf16[32,24,512]{2,1,0:T(8,128)(2,1)}), bf16[32,24,512]{2,1,0:T(8,128)(2,1)S(1)}, u32[]{:S(2)}, u32[]{:S(2)}) async-start(bf16[32,24,512]{2,1,0:T(8,128)(2,1)} %bitcast.17), calls=%async_computation.8 | async-start | bytes 1572864 | tf_op jit(solution)/shard_map/all_to_all | solution.py:28
  166.8 2.3 %fusion.5 = f32[768,512]{1,0:T(8,128)S(1)} fusion(bf16[768,512]{1,0:T(8,128)(2,1)} %copy-done, f32[768,768]{1,0:T(8,128)S(1)} %get-tuple-element.20, s32[768]{0:T(1024)S(1)} %get-tuple-element.19, f32[768]{0:T(1024)S(1)} %get-tuple-element.37, f32[768]{0:T(1024)S(1)} %multiply_divide_fusion, f32[768]{0:T(1024)S(1)} %multiply_divide_fusion.2, ...), kind=kOutput, calls=%fused_computation.21 | convolution fusion | flops 608698368 | bytes 4737024 | tf_op jit(solution)/shard_map/dot_general | solution.py:113
  169.2 3.8 %collective-permute-start = (bf16[384,512]{1,0:T(8,128)(2,1)S(1)}, bf16[384,512]{1,0:T(8,128)(2,1)S(1)}, u32[]{:S(2)}, u32[]{:S(2)}) collective-permute-start(bf16[384,512]{1,0:T(8,128)(2,1)S(1)} %dynamic-slice_convert_fusion), channel_id=1, source_target_pairs={{0,16},{16,0},{1,17},{17,1},{2,18},{18,2},{3,19},{19,3},{4,20},{20... | collective-permute-start | bytes 1179656 | tf_op jit(solution)/shard_map/ppermute | solution.py:47
  173.0 1.3 collective-permute-done
  174.5 2.4 %collective-permute-start.1 = (bf16[2,96,512]{2,1,0:T(8,128)(2,1)S(1)}, bf16[2,96,512]{2,1,0:T(8,128)(2,1)S(1)}, u32[]{:S(2)}, u32[]{:S(2)}) collective-permute-start(bf16[2,96,512]{2,1,0:T(8,128)(2,1)S(1)} %dynamic-slice_convert_fusion.1), channel_id=1, source_target_pairs={{0,4},{4,0},{1,5},{5,1},{2,6},{6,2},{3,7},{7,3},{8,12},{12,8},{9,1... | collective-permute-start | bytes 589832 | tf_op jit(solution)/shard_map/ppermute | solution.py:47
  176.9 11.4 %collective-permute-done.1 = bf16[2,96,512]{2,1,0:T(8,128)(2,1)S(1)} collective-permute-done((bf16[2,96,512]{2,1,0:T(8,128)(2,1)S(1)}, bf16[2,96,512]{2,1,0:T(8,128)(2,1)S(1)}, u32[]{:S(2)}, u32[]{:S(2)}) %collective-permute-start.1) | collective-permute-done | bytes 196640 | tf_op jit(solution)/shard_map/ppermute | solution.py:47
  188.3 0.7 add_convert_fusion
  189.2 6.9 %all-to-all-start.9 = ((bf16[8,24,512]{2,1,0:T(8,128)(2,1)}), bf16[8,24,512]{2,1,0:T(8,128)(2,1)S(1)}, u32[]{:S(2)}, u32[]{:S(2)}) async-start(bf16[8,24,512]{2,1,0:T(8,128)(2,1)} %bitcast.5), calls=%async_computation.9 | async-start | bytes 393216 | tf_op jit(solution)/shard_map/all_to_all | solution.py:28
  196.2 0.7 subtract_divide_fusion
  196.9 5.4 %all-to-all-done.9 = bf16[8,24,512]{2,1,0:T(8,128)(2,1)S(1)} async-done(((bf16[8,24,512]{2,1,0:T(8,128)(2,1)}), bf16[8,24,512]{2,1,0:T(8,128)(2,1)S(1)}, u32[]{:S(2)}, u32[]{:S(2)}) %all-to-all-start.9) | async-done | bytes 196640 | tf_op jit(solution)/shard_map/all_to_all | solution.py:28
  202.4 0.7 subtract_divide_fusion.1
  (58 shorter events, 4.3 us)
Async XLA Ops:
  0.6 15.2 %copy-start.2 = (bf16[24,512]{1,0:T(8,128)(2,1)S(1)}, bf16[24,512]{1,0:T(8,128)(2,1)}, u32[]{:S(2)}) copy-start(bf16[24,512]{1,0:T(8,128)(2,1)} %param.3) | copy-start | bytes 73732
  0.6 15.3 %copy-start.1 = (bf16[384,512]{1,0:T(8,128)(2,1)S(1)}, bf16[384,512]{1,0:T(8,128)(2,1)}, u32[]{:S(2)}) copy-start(bf16[384,512]{1,0:T(8,128)(2,1)} %param.2) | copy-start | bytes 1179652
  2.4 37.0 %all-to-all-start = ((bf16[32,24,512]{2,1,0:T(8,128)(2,1)}), bf16[32,24,512]{2,1,0:T(8,128)(2,1)S(1)}, u32[]{:S(2)}, u32[]{:S(2)}) async-start(bf16[32,24,512]{2,1,0:T(8,128)(2,1)} %broadcast_in_dim.24), calls=%async_computation | async-start | bytes 1572864 | tf_op jit(solution)/shard_map/all_to_all | solution.py:28
  40.0 1.1 copy-start
  162.9 26.2 %all-to-all-start.8 = ((bf16[32,24,512]{2,1,0:T(8,128)(2,1)}), bf16[32,24,512]{2,1,0:T(8,128)(2,1)S(1)}, u32[]{:S(2)}, u32[]{:S(2)}) async-start(bf16[32,24,512]{2,1,0:T(8,128)(2,1)} %bitcast.17), calls=%async_computation.8 | async-start | bytes 1572864 | tf_op jit(solution)/shard_map/all_to_all | solution.py:28
  169.2 5.1 %collective-permute-start = (bf16[384,512]{1,0:T(8,128)(2,1)S(1)}, bf16[384,512]{1,0:T(8,128)(2,1)S(1)}, u32[]{:S(2)}, u32[]{:S(2)}) collective-permute-start(bf16[384,512]{1,0:T(8,128)(2,1)S(1)} %dynamic-slice_convert_fusion), channel_id=1, source_target_pairs={{0,16},{16,0},{1,17},{17,1},{2,18},{18,2},{3,19},{19,3},{4,20},{20... | collective-permute-start | bytes 1179656 | tf_op jit(solution)/shard_map/ppermute | solution.py:47
  174.5 13.8 %collective-permute-start.1 = (bf16[2,96,512]{2,1,0:T(8,128)(2,1)S(1)}, bf16[2,96,512]{2,1,0:T(8,128)(2,1)S(1)}, u32[]{:S(2)}, u32[]{:S(2)}) collective-permute-start(bf16[2,96,512]{2,1,0:T(8,128)(2,1)S(1)} %dynamic-slice_convert_fusion.1), channel_id=1, source_target_pairs={{0,4},{4,0},{1,5},{5,1},{2,6},{6,2},{3,7},{7,3},{8,12},{12,8},{9,1... | collective-permute-start | bytes 589832 | tf_op jit(solution)/shard_map/ppermute | solution.py:47
  189.2 13.1 %all-to-all-start.9 = ((bf16[8,24,512]{2,1,0:T(8,128)(2,1)}), bf16[8,24,512]{2,1,0:T(8,128)(2,1)S(1)}, u32[]{:S(2)}, u32[]{:S(2)}) async-start(bf16[8,24,512]{2,1,0:T(8,128)(2,1)} %bitcast.5), calls=%async_computation.9 | async-start | bytes 393216 | tf_op jit(solution)/shard_map/all_to_all | solution.py:28

commit v5 on v4

--- a/solution.py
+++ b/solution.py
@@ -1,6 +1,7 @@
 import jax
 import jax.numpy as jnp
 from jax import lax
+from jax.experimental.layout import Layout, with_layout_constraint
 from jax.sharding import Mesh, PartitionSpec as P
 
 ROUNDS = 3
@@ -19,9 +20,9 @@
     return (wide / length, length)
 
 
-def project_back(grad, unit, length):
-    along = jnp.sum(unit * grad, axis=1, keepdims=True)
-    return (grad - unit * along) / length
+def project_out(grad, unit):
+    grad = with_layout_constraint(grad, Layout((0, 1)))
+    return grad - unit * jnp.sum(unit * grad, axis=1, keepdims=True)
 
 
 def exchange(parts, axes):
@@ -73,12 +74,12 @@
     places = [c_index * half_c, (1 - c_index) * half_c, z_index * half_z, (1 - z_index) * half_z]
     places = [place.astype(jnp.uint32) for place in places]
     own_img = lax.dynamic_slice_in_dim(images, t_index * own, own, 0)
-    own_units = normalize(own_img) + normalize(texts)
-    both, img_ids, txt_ids, places, own_units = lax.optimization_barrier(
-        (both, img_ids, txt_ids, places, own_units)
+    lengths = (normalize(own_img)[1], normalize(texts)[1])
+    both, img_ids, txt_ids, places, lengths = lax.optimization_barrier(
+        (both, img_ids, txt_ids, places, lengths)
     )
-    img_bf = normalize(both)[0].astype(jnp.bfloat16)
-    txt_bf = normalize(raw_txt)[0].astype(jnp.bfloat16)
+    unit_img, unit_txt = normalize(both)[0], normalize(raw_txt)[0]
+    img_bf, txt_bf = unit_img.astype(jnp.bfloat16), unit_txt.astype(jnp.bfloat16)
     scores = logit_scale * lax.dot_general(
         txt_bf, img_bf, (((1,), (1,)), ((), ())), preferred_element_type=jnp.float32
     )
@@ -108,18 +109,20 @@
         return grad_logit.astype(jnp.bfloat16)
 
     g_part = jnp.dot(logits(kernel), img_bf, preferred_element_type=jnp.float32)
+    g_part = project_out(g_part, unit_txt)
     g_part, kernel = lax.optimization_barrier((g_part.astype(jnp.bfloat16), kernel))
     g_txt = logit_scale * scatter_sum(g_part.reshape(-1, own, width), "p")
     g_part = lax.dot_general(
         logits(kernel), txt_bf, (((0,), (0,)), ((), ())), preferred_element_type=jnp.float32
     )
+    g_part = project_out(g_part, unit_img)
     g_part = keep_half(g_part, places[:2], "c", 0)
     g_part = g_part.reshape(NEAR, -1, width)
     g_part = keep_half(g_part, places[2:], "zh", 1).astype(jnp.bfloat16)
     g_part, g_txt = lax.optimization_barrier((g_part, g_txt))
     g_img = logit_scale * scatter_sum(g_part.reshape(-1, own, width), ("x", "zl"))
-    grad_images = project_back(g_img, *own_units[:2])
-    grad_texts = project_back(g_txt, *own_units[2:])
+    grad_images = g_img / lengths[0]
+    grad_texts = g_txt / lengths[1]
     return (grad_images, grad_texts)
 
 

time: 205 us -> 211 us (1.029)
  starting transfers between devices: 30.4 us -> 32.6 us
    all_to_all x3, starting transfers between devices: 24.2 us -> 26.4 us  [exchange(): return lax.all_to_all(parts, axes, 0, 0, tiled=True)]
  transfers between devices with their start and end apart: 5 -> 5, of which waited for: 4 -> 4; matrix products, arithmetic and copies ran while one was open for 2% -> 1% of each run, Pallas kernels for 0% -> 0%
where the time goes in v5:
time: 211 us; the launch traced here: 209 us
  blocking collectives  124 us (59%)
  waiting for transfers between devices  34 us (16%)
  starting transfers between devices  32.6 us (15%)
  matrix products  7.17 us (3%)
  other arithmetic  7.03 us (3%)
  local copies, waits for them, and re-layouts  3.32 us (2%)
    all_to_all x7, blocking collectives, exchange(): return lax.all_to_all(parts, axes, 0, 0, tiled=True)  117 us
    all_to_all x3, starting transfers between devices, exchange(): return lax.all_to_all(parts, axes, 0, 0, tiled=True)  26.4 us
    all_to_all x3, waiting for transfers between devices, exchange(): return lax.all_to_all(parts, axes, 0, 0, tiled=True)  21.3 us
    ppermute x2, waiting for transfers between devices, keep_half(): lax.ppermute(other, axis, [(0, 1), (1, 0)]).astype(jnp.float32)  12.7 us
    all_gather x1, blocking collectives, shards(): both = lax.all_gather(images, 'c', axis=0, tiled=True)  6.64 us
    ppermute x2, starting transfers between devices, keep_half(): lax.ppermute(other, axis, [(0, 1), (1, 0)]).astype(jnp.float32)  6.18 us
  transfers between devices with their start and end apart: 5, of which 4 were waited for; matrix products, arithmetic and copies ran while one was open for 1% of the time, Pallas kernels for 0%

profile of v5, /device:TPU:1, one launch (start us, length us, event | category | flops | bytes accessed | tf_op | source)
XLA Modules:
  0.0 209.0 jit_solution(1564524282027473147)
XLA Ops:
  0.6 1.7 broadcast_in_dim.24
  2.4 13.4 %all-to-all-start = ((bf16[32,24,512]{2,1,0:T(8,128)(2,1)}), bf16[32,24,512]{2,1,0:T(8,128)(2,1)S(1)}, u32[]{:S(2)}, u32[]{:S(2)}) async-start(bf16[32,24,512]{2,1,0:T(8,128)(2,1)} %broadcast_in_dim.24), calls=%async_computation | async-start | bytes 1572864 | tf_op jit(solution)/shard_map/all_to_all | solution.py:29
  16.1 6.6 %all_gather.3 = bf16[768,512]{1,0:T(8,128)(2,1)S(1)} all-gather(bf16[384,512]{1,0:T(8,128)(2,1)S(1)} %copy-done.6), channel_id=1, replica_groups=mesh['p'=32,'c'=2,'x'=2,'zh'=2,'zl'=4] {'c'}, dimensions={0}, use_global_device_ids=true | all-gather | bytes 1179648 | tf_op jit(solution)/shard_map/all_gather | solution.py:66
  23.6 15.8 %all-to-all-done = bf16[32,24,512]{2,1,0:T(8,128)(2,1)S(1)} async-done(((bf16[32,24,512]{2,1,0:T(8,128)(2,1)}), bf16[32,24,512]{2,1,0:T(8,128)(2,1)S(1)}, u32[]{:S(2)}, u32[]{:S(2)}) %all-to-all-start) | async-done | bytes 786464 | tf_op jit(solution)/shard_map/all_to_all | solution.py:29
  40.0 2.5 %fusion.43 = (f32[768]{0:T(1024)S(1)}, f32[768,768]{1,0:T(8,128)S(1)}) fusion(bf16[768,512]{1,0:T(8,128)(2,1)S(1)} %bitcast_divide_fusion, f32[768]{0:T(1024)S(1)} %add_sqrt_fusion.1, bf16[768,512]{1,0:T(8,128)(2,1)} %copy-done), kind=kOutput, calls=%fused_computation.90 | convolution fusion | flops 606928128 | bytes 3938304 | tf_op jit(solution)/shard_map/dot_general | solution.py:83
  42.5 19.4 %all_to_all.56 = f32[32,1,768]{2,1,0:T(1,128)S(1)} all-to-all(f32[32,1,768]{2,1,0:T(1,128)S(1)} %broadcast_in_dim.25), channel_id=1, replica_groups=mesh['p'=32,'c'=2,'x'=2,'zh'=2,'zl'=4] {'p'}, dimensions={0} | all-to-all | bytes 196608 | tf_op jit(solution)/shard_map/all_to_all | solution.py:29
  62.4 28.6 %all_to_all.57 = f32[32,2,768]{2,1,0:T(2,128)S(1)} all-to-all(f32[32,2,768]{2,1,0:T(2,128)S(1)} %broadcast_in_dim.26), channel_id=1, replica_groups=mesh['p'=32,'c'=2,'x'=2,'zh'=2,'zl'=4] {'c','x','zh','zl'}, dimensions={0} | all-to-all | bytes 393216 | tf_op jit(solution)/shard_map/all_to_all | solution.py:29
  91.4 14.5 %all_to_all.58 = f32[32,1,768]{2,1,0:T(1,128)S(1)} all-to-all(f32[32,1,768]{2,1,0:T(1,128)S(1)} %broadcast_in_dim.27), channel_id=1, replica_groups=mesh['p'=32,'c'=2,'x'=2,'zh'=2,'zl'=4] {'p'}, dimensions={0} | all-to-all | bytes 196608 | tf_op jit(solution)/shard_map/all_to_all | solution.py:29
  106.3 13.0 %all_to_all.59 = f32[32,1,768]{2,1,0:T(1,128)S(1)} all-to-all(f32[32,1,768]{2,1,0:T(1,128)S(1)} %broadcast_in_dim.28), channel_id=1, replica_groups=mesh['p'=32,'c'=2,'x'=2,'zh'=2,'zl'=4] {'c','x','zh','zl'}, dimensions={0} | all-to-all | bytes 196608 | tf_op jit(solution)/shard_map/all_to_all | solution.py:29
  119.7 14.4 %all_to_all.60 = f32[32,1,768]{2,1,0:T(1,128)S(1)} all-to-all(f32[32,1,768]{2,1,0:T(1,128)S(1)} %broadcast_in_dim.29), channel_id=1, replica_groups=mesh['p'=32,'c'=2,'x'=2,'zh'=2,'zl'=4] {'p'}, dimensions={0} | all-to-all | bytes 196608 | tf_op jit(solution)/shard_map/all_to_all | solution.py:29
  134.5 12.9 %all_to_all.61 = f32[32,1,768]{2,1,0:T(1,128)S(1)} all-to-all(f32[32,1,768]{2,1,0:T(1,128)S(1)} %broadcast_in_dim.30), channel_id=1, replica_groups=mesh['p'=32,'c'=2,'x'=2,'zh'=2,'zl'=4] {'c','x','zh','zl'}, dimensions={0} | all-to-all | bytes 196608 | tf_op jit(solution)/shard_map/all_to_all | solution.py:29
  147.8 14.4 %all_to_all.62 = f32[32,1,768]{2,1,0:T(1,128)S(1)} all-to-all(f32[32,1,768]{2,1,0:T(1,128)S(1)} %broadcast_in_dim.31), channel_id=1, replica_groups=mesh['p'=32,'c'=2,'x'=2,'zh'=2,'zl'=4] {'p'}, dimensions={0} | all-to-all | bytes 196608 | tf_op jit(solution)/shard_map/all_to_all | solution.py:29
  162.3 2.3 %multiply_reduce_fusion.7 = (f32[768]{0:T(1024)S(1)}, f32[768,512]{1,0:T(8,128)S(1)}) fusion(f32[768]{0:T(1024)S(1)} %sqrt.48, bf16[32,24,512]{2,1,0:T(8,128)(2,1)S(1)} %all-to-all-done, f32[768]{0:T(1024)S(1)} %add_sqrt_fusion.1, bf16[768,512]{1,0:T(8,128)(2,1)} %copy-done, f32[768,768]{1,0:T(8,128)S(1)} %get-tuple-element.18, ...), kind=kOutput, calls=%fused_computation.20 | convolution fusion | flops 611450112 | bytes 5532672 | tf_op jit(solution)/shard_map/dot_general | solution.py:111
  164.7 1.3 subtract_convert_fusion
  166.3 2.4 %multiply_reduce_fusion.6 = (f32[768]{0:T(1024)S(1)}, f32[768,512]{1,0:T(8,128)}) fusion(f32[768]{0:T(1024)S(1)} %add_sqrt_fusion.1, bf16[768,512]{1,0:T(8,128)(2,1)S(1)} %copy-done.1, bf16[768,512]{1,0:T(8,128)(2,1)S(1)} %copy-done.5, f32[768,768]{1,0:T(8,128)S(1)} %get-tuple-element.18, s32[768]{0:T(1024)S(1)} %get-tuple-element.17, ...), kind=kOutput, calls=%fused_computation.18 | convolution fusion | flops 610270464 | bytes 5529600 | tf_op jit(solution)/shard_map/dot_general | solution.py:115
  168.6 4.0 %all-to-all-start.8 = ((bf16[32,24,512]{2,1,0:T(8,128)(2,1)}), bf16[32,24,512]{2,1,0:T(8,128)(2,1)S(1)}, u32[]{:S(2)}, u32[]{:S(2)}) async-start(bf16[32,24,512]{2,1,0:T(8,128)(2,1)} %bitcast.17), calls=%async_computation.8 | async-start | bytes 1572864 | tf_op jit(solution)/shard_map/all_to_all | solution.py:29
  173.1 3.8 %collective-permute-start = (bf16[384,512]{1,0:T(8,128)(2,1)S(1)}, bf16[384,512]{1,0:T(8,128)(2,1)S(1)}, u32[]{:S(2)}, u32[]{:S(2)}) collective-permute-start(bf16[384,512]{1,0:T(8,128)(2,1)S(1)} %dynamic-slice_convert_fusion), channel_id=1, source_target_pairs={{0,16},{16,0},{1,17},{17,1},{2,18},{18,2},{3,19},{19,3},{4,20},{20... | collective-permute-start | bytes 1179656 | tf_op jit(solution)/shard_map/ppermute | solution.py:48
  176.9 1.3 collective-permute-done
  178.4 2.4 %collective-permute-start.1 = (bf16[2,96,512]{2,1,0:T(8,128)(2,1)S(1)}, bf16[2,96,512]{2,1,0:T(8,128)(2,1)S(1)}, u32[]{:S(2)}, u32[]{:S(2)}) collective-permute-start(bf16[2,96,512]{2,1,0:T(8,128)(2,1)S(1)} %dynamic-slice_convert_fusion.1), channel_id=1, source_target_pairs={{0,4},{4,0},{1,5},{5,1},{2,6},{6,2},{3,7},{7,3},{8,12},{12,8},{9,1... | collective-permute-start | bytes 589832 | tf_op jit(solution)/shard_map/ppermute | solution.py:48
  180.9 11.4 %collective-permute-done.1 = bf16[2,96,512]{2,1,0:T(8,128)(2,1)S(1)} collective-permute-done((bf16[2,96,512]{2,1,0:T(8,128)(2,1)S(1)}, bf16[2,96,512]{2,1,0:T(8,128)(2,1)S(1)}, u32[]{:S(2)}, u32[]{:S(2)}) %collective-permute-start.1) | collective-permute-done | bytes 196640 | tf_op jit(solution)/shard_map/ppermute | solution.py:48
  192.2 0.7 add_convert_fusion
  193.1 9.0 %all-to-all-start.9 = ((bf16[8,24,512]{2,1,0:T(8,128)(2,1)}), bf16[8,24,512]{2,1,0:T(8,128)(2,1)S(1)}, u32[]{:S(2)}, u32[]{:S(2)}) async-start(bf16[8,24,512]{2,1,0:T(8,128)(2,1)} %bitcast.5), calls=%async_computation.9 | async-start | bytes 393216 | tf_op jit(solution)/shard_map/all_to_all | solution.py:29
  202.8 5.5 %all-to-all-done.9 = bf16[8,24,512]{2,1,0:T(8,128)(2,1)S(1)} async-done(((bf16[8,24,512]{2,1,0:T(8,128)(2,1)}), bf16[8,24,512]{2,1,0:T(8,128)(2,1)S(1)}, u32[]{:S(2)}, u32[]{:S(2)}) %all-to-all-start.9) | async-done | bytes 196640 | tf_op jit(solution)/shard_map/all_to_all | solution.py:29
  208.3 0.7 multiply_divide_fusion
  (66 shorter events, 5.9 us)
Async XLA Ops:
  0.6 15.3 %copy-start.7 = (bf16[24,512]{1,0:T(8,128)(2,1)S(1)}, bf16[24,512]{1,0:T(8,128)(2,1)}, u32[]{:S(2)}) copy-start(bf16[24,512]{1,0:T(8,128)(2,1)} %param.3) | copy-start | bytes 73732
  0.6 15.2 %copy-start.6 = (bf16[384,512]{1,0:T(8,128)(2,1)S(1)}, bf16[384,512]{1,0:T(8,128)(2,1)}, u32[]{:S(2)}) copy-start(bf16[384,512]{1,0:T(8,128)(2,1)} %param.2) | copy-start | bytes 1179652
  2.4 37.0 %all-to-all-start = ((bf16[32,24,512]{2,1,0:T(8,128)(2,1)}), bf16[32,24,512]{2,1,0:T(8,128)(2,1)S(1)}, u32[]{:S(2)}, u32[]{:S(2)}) async-start(bf16[32,24,512]{2,1,0:T(8,128)(2,1)} %broadcast_in_dim.24), calls=%async_computation | async-start | bytes 1572864 | tf_op jit(solution)/shard_map/all_to_all | solution.py:29
  22.7 0.9 copy-start
  40.0 2.5 %copy-start.4 = (bf16[768,512]{1,0:T(8,128)(2,1)}, bf16[768,512]{1,0:T(8,128)(2,1)S(1)}, u32[]{:S(2)}) copy-start(bf16[768,512]{1,0:T(8,128)(2,1)S(1)} %bitcast_divide_fusion) | copy-start | bytes 2359300
  164.7 1.3 copy-start.1
  164.7 1.6 copy-start.5
  166.2 6.4 %copy-start.2 = (bf16[768,512]{1,0:T(8,128)(2,1)S(1)}, bf16[768,512]{1,0:T(8,128)(2,1)}, u32[]{:S(2)}) copy-start(bf16[768,512]{1,0:T(8,128)(2,1)} %copy-done) | copy-start | bytes 2359300
  168.6 4.1 %copy-start.3 = (f32[768,512]{1,0:T(8,128)S(1)}, f32[768,512]{1,0:T(8,128)}, u32[]{:S(2)}) copy-start(f32[768,512]{1,0:T(8,128)} %get-tuple-element.39) | copy-start | bytes 4718596
  168.6 24.3 %all-to-all-start.8 = ((bf16[32,24,512]{2,1,0:T(8,128)(2,1)}), bf16[32,24,512]{2,1,0:T(8,128)(2,1)S(1)}, u32[]{:S(2)}, u32[]{:S(2)}) async-start(bf16[32,24,512]{2,1,0:T(8,128)(2,1)} %bitcast.17), calls=%async_computation.8 | async-start | bytes 1572864 | tf_op jit(solution)/shard_map/all_to_all | solution.py:29
  173.1 5.1 %collective-permute-start = (bf16[384,512]{1,0:T(8,128)(2,1)S(1)}, bf16[384,512]{1,0:T(8,128)(2,1)S(1)}, u32[]{:S(2)}, u32[]{:S(2)}) collective-permute-start(bf16[384,512]{1,0:T(8,128)(2,1)S(1)} %dynamic-slice_convert_fusion), channel_id=1, source_target_pairs={{0,16},{16,0},{1,17},{17,1},{2,18},{18,2},{3,19},{19,3},{4,20},{20... | collective-permute-start | bytes 1179656 | tf_op jit(solution)/shard_map/ppermute | solution.py:48
  178.4 13.8 %collective-permute-start.1 = (bf16[2,96,512]{2,1,0:T(8,128)(2,1)S(1)}, bf16[2,96,512]{2,1,0:T(8,128)(2,1)S(1)}, u32[]{:S(2)}, u32[]{:S(2)}) collective-permute-start(bf16[2,96,512]{2,1,0:T(8,128)(2,1)S(1)} %dynamic-slice_convert_fusion.1), channel_id=1, source_target_pairs={{0,4},{4,0},{1,5},{5,1},{2,6},{6,2},{3,7},{7,3},{8,12},{12,8},{9,1... | collective-permute-start | bytes 589832 | tf_op jit(solution)/shard_map/ppermute | solution.py:48
  193.1 15.2 %all-to-all-start.9 = ((bf16[8,24,512]{2,1,0:T(8,128)(2,1)}), bf16[8,24,512]{2,1,0:T(8,128)(2,1)S(1)}, u32[]{:S(2)}, u32[]{:S(2)}) async-start(bf16[8,24,512]{2,1,0:T(8,128)(2,1)} %bitcast.5), calls=%async_computation.9 | async-start | bytes 393216 | tf_op jit(solution)/shard_map/all_to_all | solution.py:29

commit v6 on v5

--- a/solution.py
+++ b/solution.py
@@ -78,7 +78,8 @@
     both, img_ids, txt_ids, places, lengths = lax.optimization_barrier(
         (both, img_ids, txt_ids, places, lengths)
     )
-    unit_img, unit_txt = normalize(both)[0], normalize(raw_txt)[0]
+    unit_img, len_img = normalize(both)
+    unit_txt, len_txt = normalize(raw_txt)
     img_bf, txt_bf = unit_img.astype(jnp.bfloat16), unit_txt.astype(jnp.bfloat16)
     scores = logit_scale * lax.dot_general(
         txt_bf, img_bf, (((1,), (1,)), ((), ())), preferred_element_type=jnp.float32
@@ -96,6 +97,9 @@
             row_sum = total_over(row_part, rows)
         row_weight = 1.0 / (total * row_sum)
         col_sum = total_over(jnp.sum(kernel * row_weight[None, :], axis=1), "p")
+    kept = (both, len_img, raw_txt, len_txt, row_weight)
+    both, len_img, raw_txt, len_txt, row_weight = lax.optimization_barrier(kept)
+    unit_img, unit_txt = both.astype(jnp.float32) / len_img, raw_txt.astype(jnp.float32) / len_txt
     col_weight = 1.0 - mix_weight + mix_weight * total * col_scale * col_sum
     by_row = 0.5 / row_total
     by_col = 0.5 * col_weight / col_total

time: 211 us -> 213 us (level)
  blocking collectives: 124 us -> 96.6 us
  waiting for transfers between devices: 34 us -> 53.6 us
  starting transfers between devices: 32.6 us -> 39.5 us
    all_to_all x7 -> x5, blocking collectives: 117 us -> 89.9 us  [exchange(): return lax.all_to_all(parts, axes, 0, 0, tiled=True)]
    all_to_all x3 -> x5, waiting for transfers between devices: 21.3 us -> 40.7 us  [exchange(): return lax.all_to_all(parts, axes, 0, 0, tiled=True)]
    all_to_all x3 -> x5, starting transfers between devices: 26.4 us -> 33.3 us  [exchange(): return lax.all_to_all(parts, axes, 0, 0, tiled=True)]
  transfers between devices with their start and end apart: 5 -> 7, of which waited for: 4 -> 6; matrix products, arithmetic and copies ran while one was open for 1% -> 3% of each run, Pallas kernels for 0% -> 0%
where the time goes in v6:
time: 213 us; the launch traced here: 211 us
  blocking collectives  96.6 us (45%)
  waiting for transfers between devices  53.6 us (25%)
  starting transfers between devices  39.5 us (19%)
  other arithmetic  8.21 us (4%)
  matrix products  7.5 us (4%)
  local copies, waits for them, and re-layouts  4.35 us (2%)
    all_to_all x5, blocking collectives, exchange(): return lax.all_to_all(parts, axes, 0, 0, tiled=True)  89.9 us
    all_to_all x5, waiting for transfers between devices, exchange(): return lax.all_to_all(parts, axes, 0, 0, tiled=True)  40.7 us
    all_to_all x5, starting transfers between devices, exchange(): return lax.all_to_all(parts, axes, 0, 0, tiled=True)  33.3 us
    ppermute x2, waiting for transfers between devices, keep_half(): lax.ppermute(other, axis, [(0, 1), (1, 0)]).astype(jnp.float32)  12.9 us
    all_gather x1, blocking collectives, shards(): both = lax.all_gather(images, 'c', axis=0, tiled=True)  6.64 us
    ppermute x2, starting transfers between devices, keep_half(): lax.ppermute(other, axis, [(0, 1), (1, 0)]).astype(jnp.float32)  6.23 us
  transfers between devices with their start and end apart: 7, of which 6 were waited for; matrix products, arithmetic and copies ran while one was open for 3% of the time, Pallas kernels for 0%

profile of v6, /device:TPU:1, one launch (start us, length us, event | category | flops | bytes accessed | tf_op | source)
XLA Modules:
  0.0 210.7 jit_solution(916233513006493013)
XLA Ops:
  0.6 1.7 broadcast_in_dim.24
  2.4 13.4 %all-to-all-start = ((bf16[32,24,512]{2,1,0:T(8,128)(2,1)}), bf16[32,24,512]{2,1,0:T(8,128)(2,1)S(1)}, u32[]{:S(2)}, u32[]{:S(2)}) async-start(bf16[32,24,512]{2,1,0:T(8,128)(2,1)} %broadcast_in_dim.24), calls=%async_computation | async-start | bytes 1572864 | tf_op jit(solution)/shard_map/all_to_all | solution.py:29
  16.1 6.6 %all_gather.3 = bf16[768,512]{1,0:T(8,128)(2,1)S(1)} all-gather(bf16[384,512]{1,0:T(8,128)(2,1)S(1)} %copy-done.3), channel_id=1, replica_groups=mesh['p'=32,'c'=2,'x'=2,'zh'=2,'zl'=4] {'c'}, dimensions={0}, use_global_device_ids=true | all-gather | bytes 1179648 | tf_op jit(solution)/shard_map/all_gather | solution.py:66
  23.6 15.8 %all-to-all-done = bf16[32,24,512]{2,1,0:T(8,128)(2,1)S(1)} async-done(((bf16[32,24,512]{2,1,0:T(8,128)(2,1)}), bf16[32,24,512]{2,1,0:T(8,128)(2,1)S(1)}, u32[]{:S(2)}, u32[]{:S(2)}) %all-to-all-start) | async-done | bytes 786464 | tf_op jit(solution)/shard_map/all_to_all | solution.py:29
  40.0 2.5 %fusion.42 = (f32[768]{0:T(1024)S(1)}, f32[768,768]{1,0:T(8,128)S(1)}) fusion(bf16[768,512]{1,0:T(8,128)(2,1)S(1)} %divide_convert_fusion, bf16[768,512]{1,0:T(8,128)(2,1)} %copy-done, f32[768]{0:T(1024)S(1)} %add_sqrt_fusion.1), kind=kOutput, calls=%fused_computation.89 | convolution fusion | flops 606928128 | bytes 3938304 | tf_op jit(solution)/shard_map/dot_general | solution.py:84
  42.5 19.4 %all_to_all.56 = f32[32,1,768]{2,1,0:T(1,128)S(1)} all-to-all(f32[32,1,768]{2,1,0:T(1,128)S(1)} %broadcast_in_dim.25), channel_id=1, replica_groups=mesh['p'=32,'c'=2,'x'=2,'zh'=2,'zl'=4] {'p'}, dimensions={0} | all-to-all | bytes 196608 | tf_op jit(solution)/shard_map/all_to_all | solution.py:29
  62.4 28.6 %all_to_all.57 = f32[32,2,768]{2,1,0:T(2,128)S(1)} all-to-all(f32[32,2,768]{2,1,0:T(2,128)S(1)} %broadcast_in_dim.26), channel_id=1, replica_groups=mesh['p'=32,'c'=2,'x'=2,'zh'=2,'zl'=4] {'c','x','zh','zl'}, dimensions={0} | all-to-all | bytes 393216 | tf_op jit(solution)/shard_map/all_to_all | solution.py:29
  91.4 14.5 %all_to_all.58 = f32[32,1,768]{2,1,0:T(1,128)S(1)} all-to-all(f32[32,1,768]{2,1,0:T(1,128)S(1)} %broadcast_in_dim.27), channel_id=1, replica_groups=mesh['p'=32,'c'=2,'x'=2,'zh'=2,'zl'=4] {'p'}, dimensions={0} | all-to-all | bytes 196608 | tf_op jit(solution)/shard_map/all_to_all | solution.py:29
  106.3 13.0 %all_to_all.59 = f32[32,1,768]{2,1,0:T(1,128)S(1)} all-to-all(f32[32,1,768]{2,1,0:T(1,128)S(1)} %broadcast_in_dim.28), channel_id=1, replica_groups=mesh['p'=32,'c'=2,'x'=2,'zh'=2,'zl'=4] {'c','x','zh','zl'}, dimensions={0} | all-to-all | bytes 196608 | tf_op jit(solution)/shard_map/all_to_all | solution.py:29
  119.7 14.4 %all_to_all.60 = f32[32,1,768]{2,1,0:T(1,128)S(1)} all-to-all(f32[32,1,768]{2,1,0:T(1,128)S(1)} %broadcast_in_dim.29), channel_id=1, replica_groups=mesh['p'=32,'c'=2,'x'=2,'zh'=2,'zl'=4] {'p'}, dimensions={0} | all-to-all | bytes 196608 | tf_op jit(solution)/shard_map/all_to_all | solution.py:29
  135.1 5.4 %all-to-all-start.6 = ((f32[32,1,768]{2,1,0:T(1,128)}), f32[32,1,768]{2,1,0:T(1,128)S(1)}, u32[]{:S(2)}, u32[]{:S(2)}) async-start(f32[32,1,768]{2,1,0:T(1,128)} %broadcast_in_dim.30), calls=%async_computation.6 | async-start | bytes 196608 | tf_op jit(solution)/shard_map/all_to_all | solution.py:29
  140.7 8.0 %all-to-all-done.6 = f32[32,1,768]{2,1,0:T(1,128)S(1)} async-done(((f32[32,1,768]{2,1,0:T(1,128)}), f32[32,1,768]{2,1,0:T(1,128)S(1)}, u32[]{:S(2)}, u32[]{:S(2)}) %all-to-all-start.6) | async-done | bytes 98336 | tf_op jit(solution)/shard_map/all_to_all | solution.py:29
  149.7 3.8 %all-to-all-start.7 = ((f32[32,1,768]{2,1,0:T(1,128)}), f32[32,1,768]{2,1,0:T(1,128)S(1)}, u32[]{:S(2)}, u32[]{:S(2)}) async-start(f32[32,1,768]{2,1,0:T(1,128)} %broadcast_in_dim.31), calls=%async_computation.7 | async-start | bytes 196608 | tf_op jit(solution)/shard_map/all_to_all | solution.py:29
  153.6 11.4 %all-to-all-done.7 = f32[32,1,768]{2,1,0:T(1,128)S(1)} async-done(((f32[32,1,768]{2,1,0:T(1,128)}), f32[32,1,768]{2,1,0:T(1,128)S(1)}, u32[]{:S(2)}, u32[]{:S(2)}) %all-to-all-start.7) | async-done | bytes 98336 | tf_op jit(solution)/shard_map/all_to_all | solution.py:29
  165.1 2.3 %multiply_reduce_fusion.7 = (f32[768]{0:T(1024)S(1)}, f32[768,512]{1,0:T(8,128)S(1)}) fusion(bf16[768,512]{1,0:T(8,128)(2,1)S(1)} %bitcast.13, f32[768]{0:T(1024)S(1)} %reduce.9, bf16[768,512]{1,0:T(8,128)(2,1)} %copy-done, f32[768]{0:T(1024)S(1)} %add_sqrt_fusion.1, f32[768,768]{1,0:T(8,128)S(1)} %get-tuple-element.26, s32[768]{0:T(1024)S(1)} %get-tuple-element.23, ...), kind=kOutput, calls=%fused_computation.21 | convolution fusion | flops 611450112 | bytes 5532672 | tf_op jit(solution)/shard_map/dot_general | solution.py:115
  168.6 4.6 %all-to-all-start.8 = ((bf16[32,24,512]{2,1,0:T(8,128)(2,1)}), bf16[32,24,512]{2,1,0:T(8,128)(2,1)}, u32[]{:S(2)}, u32[]{:S(2)}) async-start(bf16[32,24,512]{2,1,0:T(8,128)(2,1)} %bitcast.15), calls=%async_computation.8 | async-start | bytes 1572864 | tf_op jit(solution)/shard_map/all_to_all | solution.py:29
  173.3 2.7 %multiply_reduce_fusion.6 = (f32[768]{0:T(1024)S(1)}, f32[768,512]{1,0:T(8,128)S(1)}) fusion(bf16[768,512]{1,0:T(8,128)(2,1)} %copy-done, f32[768]{0:T(1024)S(1)} %reduce.10, bf16[768,512]{1,0:T(8,128)(2,1)} %copy-done.2, f32[768,768]{1,0:T(8,128)S(1)} %get-tuple-element.26, s32[768]{0:T(1024)S(1)} %get-tuple-element.23, ...), kind=kOutput, calls=%fused_computation.18 | convolution fusion | flops 610270464 | bytes 5529600 | tf_op jit(solution)/shard_map/dot_general | solution.py:119
  176.4 3.8 %collective-permute-start = (bf16[384,512]{1,0:T(8,128)(2,1)S(1)}, bf16[384,512]{1,0:T(8,128)(2,1)S(1)}, u32[]{:S(2)}, u32[]{:S(2)}) collective-permute-start(bf16[384,512]{1,0:T(8,128)(2,1)S(1)} %dynamic-slice_convert_fusion), channel_id=1, source_target_pairs={{0,16},{16,0},{1,17},{17,1},{2,18},{18,2},{3,19},{19,3},{4,20},{20... | collective-permute-start | bytes 1179656 | tf_op jit(solution)/shard_map/ppermute | solution.py:48
  180.2 1.3 collective-permute-done
  181.7 2.5 %collective-permute-start.1 = (bf16[2,96,512]{2,1,0:T(8,128)(2,1)S(1)}, bf16[2,96,512]{2,1,0:T(8,128)(2,1)S(1)}, u32[]{:S(2)}, u32[]{:S(2)}) collective-permute-start(bf16[2,96,512]{2,1,0:T(8,128)(2,1)S(1)} %dynamic-slice_convert_fusion.1), channel_id=1, source_target_pairs={{0,4},{4,0},{1,5},{5,1},{2,6},{6,2},{3,7},{7,3},{8,12},{12,8},{9,1... | collective-permute-start | bytes 589832 | tf_op jit(solution)/shard_map/ppermute | solution.py:48
  184.2 11.6 %collective-permute-done.1 = bf16[2,96,512]{2,1,0:T(8,128)(2,1)S(1)} collective-permute-done((bf16[2,96,512]{2,1,0:T(8,128)(2,1)S(1)}, bf16[2,96,512]{2,1,0:T(8,128)(2,1)S(1)}, u32[]{:S(2)}, u32[]{:S(2)}) %collective-permute-start.1) | collective-permute-done | bytes 196640 | tf_op jit(solution)/shard_map/ppermute | solution.py:48
  196.5 1.3 convert_reduce_fusion
  197.8 5.9 %all-to-all-start.9 = ((bf16[8,24,512]{2,1,0:T(8,128)(2,1)}), bf16[8,24,512]{2,1,0:T(8,128)(2,1)S(1)}, u32[]{:S(2)}, u32[]{:S(2)}) async-start(bf16[8,24,512]{2,1,0:T(8,128)(2,1)} %bitcast.5), calls=%async_computation.9 | async-start | bytes 393216 | tf_op jit(solution)/shard_map/all_to_all | solution.py:29
  204.4 5.5 %all-to-all-done.9 = bf16[8,24,512]{2,1,0:T(8,128)(2,1)S(1)} async-done(((bf16[8,24,512]{2,1,0:T(8,128)(2,1)}), bf16[8,24,512]{2,1,0:T(8,128)(2,1)S(1)}, u32[]{:S(2)}, u32[]{:S(2)}) %all-to-all-start.9) | async-done | bytes 196640 | tf_op jit(solution)/shard_map/all_to_all | solution.py:29
  (67 shorter events, 9.6 us)
Async XLA Ops:
  0.6 15.4 %copy-start.4 = (bf16[24,512]{1,0:T(8,128)(2,1)S(1)}, bf16[24,512]{1,0:T(8,128)(2,1)}, u32[]{:S(2)}) copy-start(bf16[24,512]{1,0:T(8,128)(2,1)} %param.3) | copy-start | bytes 73732
  0.6 15.2 %copy-start.3 = (bf16[384,512]{1,0:T(8,128)(2,1)S(1)}, bf16[384,512]{1,0:T(8,128)(2,1)}, u32[]{:S(2)}) copy-start(bf16[384,512]{1,0:T(8,128)(2,1)} %param.2) | copy-start | bytes 1179652
  2.4 37.0 %all-to-all-start = ((bf16[32,24,512]{2,1,0:T(8,128)(2,1)}), bf16[32,24,512]{2,1,0:T(8,128)(2,1)S(1)}, u32[]{:S(2)}, u32[]{:S(2)}) async-start(bf16[32,24,512]{2,1,0:T(8,128)(2,1)} %broadcast_in_dim.24), calls=%async_computation | async-start | bytes 1572864 | tf_op jit(solution)/shard_map/all_to_all | solution.py:29
  22.8 0.9 copy-start
  40.0 2.5 %copy-start.2 = (bf16[768,512]{1,0:T(8,128)(2,1)}, bf16[768,512]{1,0:T(8,128)(2,1)S(1)}, u32[]{:S(2)}) copy-start(bf16[768,512]{1,0:T(8,128)(2,1)S(1)} %divide_convert_fusion) | copy-start | bytes 2359300
  135.1 13.5 %all-to-all-start.6 = ((f32[32,1,768]{2,1,0:T(1,128)}), f32[32,1,768]{2,1,0:T(1,128)S(1)}, u32[]{:S(2)}, u32[]{:S(2)}) async-start(f32[32,1,768]{2,1,0:T(1,128)} %broadcast_in_dim.30), calls=%async_computation.6 | async-start | bytes 196608 | tf_op jit(solution)/shard_map/all_to_all | solution.py:29
  149.7 15.3 %all-to-all-start.7 = ((f32[32,1,768]{2,1,0:T(1,128)}), f32[32,1,768]{2,1,0:T(1,128)S(1)}, u32[]{:S(2)}, u32[]{:S(2)}) async-start(f32[32,1,768]{2,1,0:T(1,128)} %broadcast_in_dim.31), calls=%async_computation.7 | async-start | bytes 196608 | tf_op jit(solution)/shard_map/all_to_all | solution.py:29
  168.6 27.9 %all-to-all-start.8 = ((bf16[32,24,512]{2,1,0:T(8,128)(2,1)}), bf16[32,24,512]{2,1,0:T(8,128)(2,1)}, u32[]{:S(2)}, u32[]{:S(2)}) async-start(bf16[32,24,512]{2,1,0:T(8,128)(2,1)} %bitcast.15), calls=%async_computation.8 | async-start | bytes 1572864 | tf_op jit(solution)/shard_map/all_to_all | solution.py:29
  173.3 2.7 %copy-start.1 = (bf16[768,512]{1,0:T(8,128)(2,1)S(1)}, bf16[768,512]{1,0:T(8,128)(2,1)}, u32[]{:S(2)}) copy-start(bf16[768,512]{1,0:T(8,128)(2,1)} %copy-done) | copy-start | bytes 2359300
  176.4 5.1 %collective-permute-start = (bf16[384,512]{1,0:T(8,128)(2,1)S(1)}, bf16[384,512]{1,0:T(8,128)(2,1)S(1)}, u32[]{:S(2)}, u32[]{:S(2)}) collective-permute-start(bf16[384,512]{1,0:T(8,128)(2,1)S(1)} %dynamic-slice_convert_fusion), channel_id=1, source_target_pairs={{0,16},{16,0},{1,17},{17,1},{2,18},{18,2},{3,19},{19,3},{4,20},{20... | collective-permute-start | bytes 1179656 | tf_op jit(solution)/shard_map/ppermute | solution.py:48
  181.7 14.1 %collective-permute-start.1 = (bf16[2,96,512]{2,1,0:T(8,128)(2,1)S(1)}, bf16[2,96,512]{2,1,0:T(8,128)(2,1)S(1)}, u32[]{:S(2)}, u32[]{:S(2)}) collective-permute-start(bf16[2,96,512]{2,1,0:T(8,128)(2,1)S(1)} %dynamic-slice_convert_fusion.1), channel_id=1, source_target_pairs={{0,4},{4,0},{1,5},{5,1},{2,6},{6,2},{3,7},{7,3},{8,12},{12,8},{9,1... | collective-permute-start | bytes 589832 | tf_op jit(solution)/shard_map/ppermute | solution.py:48
  197.8 12.1 %all-to-all-start.9 = ((bf16[8,24,512]{2,1,0:T(8,128)(2,1)}), bf16[8,24,512]{2,1,0:T(8,128)(2,1)S(1)}, u32[]{:S(2)}, u32[]{:S(2)}) async-start(bf16[8,24,512]{2,1,0:T(8,128)(2,1)} %bitcast.5), calls=%async_computation.9 | async-start | bytes 393216 | tf_op jit(solution)/shard_map/all_to_all | solution.py:29
